TPU v7x, 32 devices: a whole 2x2x4 slice. The times are simulated.
32 devices in a mesh: dp: 8 (over z, core), clus: 4 (over y, x).
Axes of the slice: x: 2, y: 2, z: 4, core: 2. Of those that a mesh axis runs over, the one named last changes fastest.
Arguments:
- rows: bfloat16 [8192, 1024], P(('dp', 'clus')), may hold values from -8 to 8
- fine_assign: int32 [8192], P(('dp', 'clus')), may hold values from 0 to 8191, as said below
- parent1: int32 [8192], P(('dp', 'clus')), may hold values from 0 to 2047, as said below
- parent2: int32 [2048], P('dp'), may hold values from 0 to 511
- parent3: int32 [512], replicated, may hold values from 0 to 63
- shrink: float32 [4], replicated, may hold values from 0.5 to 2
Outputs:
- fine_centroids: bfloat16 [8192, 1024], P(('dp', 'clus'))
- mid_centroids: bfloat16 [2048, 1024], P(('dp', 'clus'))
- coarse_centroids: bfloat16 [512, 1024], P(('dp', 'clus'))
- spread: float32 [8192], P(('dp', 'clus'))
Inputs may be any that keep to these rules, and one draw needn't show every extreme that they name: `fine_assign`: devices are numbered d = dp index * 4 + clus index, and fine centroid k is owned by device k // 256. Every row of device d names a fine centroid owned by a device of the same dp index. At most 128 rows of one device name centroids of one owner, and in every dp group some owner is named by exactly 128 rows of each device of the group. parent1[k] is one of the 256 second-level centroids g * 256 to g * 256 + 255, with g = k // 1024.
All inputs are finite; a program needn't handle non-finite values.
Results may differ from a plain program's by a relative error of at most 0.0035.
Values may be sent and summed in bfloat16 or wider, within the bound.
A program may use at most 64 MiB of HBM per device.

v0:
```python
import functools

import jax
import jax.numpy as jnp
from jax import lax
from jax.experimental import pallas as pl
from jax.experimental.pallas import tpu as pltpu
from jax.sharding import PartitionSpec as P

K4 = 64


HIGH = lax.Precision.HIGHEST


def shrunk(sums, counts, prior, weight):
    return (sums + weight * prior) / (counts + weight)[:, None]


def local(rows, fine_assign, parent1, parent2, parent3, shrink):
    groups = lax.axis_size("clus")
    dp_count = lax.axis_size("dp")
    devices = groups * dp_count
    clus_index = lax.axis_index("clus")
    dp_index = lax.axis_index("dp")
    count = rows.shape[0]
    width = rows.shape[1]
    fine_dev = parent1.shape[0]
    middle_dp = parent2.shape[0]
    third = parent3.shape[0]
    slots = 2 * count // groups
    total = count * devices
    weight_top = shrink[0] * (total / K4)
    weight_third = shrink[1] * (total / third)
    weight_middle = shrink[2] * (total / (middle_dp * dp_count))
    weight_fine = shrink[3] * (total / (fine_dev * devices))
    local_ids = fine_assign - dp_index * groups * fine_dev
    target = local_ids // fine_dev
    within = local_ids - target * fine_dev
    target_hot = (target[:, None] == jnp.arange(groups)[None, :]).astype(jnp.bfloat16)
    earlier = (jnp.arange(count)[:, None] > jnp.arange(count)[None, :]).astype(jnp.bfloat16)
    before = jnp.dot(earlier, target_hot, preferred_element_type=jnp.float32)
    rank = jnp.sum(before * target_hot.astype(jnp.float32), axis=1).astype(jnp.int32)
    slot_of = target * slots + rank
    source = (
        jnp.full((groups * slots,), count, jnp.int32)
        .at[slot_of]
        .set(jnp.arange(count, dtype=jnp.int32))
    )
    padded = jnp.concatenate([rows, jnp.zeros((1, width), jnp.bfloat16)], axis=0)
    send_rows = padded[source].reshape(groups, slots, width)
    send_ids = jnp.concatenate([within, jnp.full((1,), -1, jnp.int32)])[source].reshape(
        groups, slots
    )
    got_rows, got_ids = (
        lax.all_to_all(send_rows, "clus", split_axis=0, concat_axis=0, tiled=True),
        lax.all_to_all(send_ids, "clus", split_axis=0, concat_axis=0, tiled=True),
    )
    got_rows = got_rows.reshape(groups * slots, width)
    got_ids = got_ids.reshape(groups * slots)
    member = (got_ids[:, None] == jnp.arange(fine_dev)[None, :]).astype(jnp.bfloat16)
    contract = (((0,), (0,)), ((), ()))
    fine_sums = lax.dot_general(member, got_rows, contract, preferred_element_type=jnp.float32)
    fine_counts = jnp.sum(member.astype(jnp.float32), axis=0)
    middle_local = parent1 - dp_index * middle_dp
    child_hot = (jnp.arange(middle_dp)[:, None] == middle_local[None, :]).astype(jnp.float32)
    middle_part = jnp.dot(child_hot, fine_sums, precision=HIGH)
    middle_tally = jnp.dot(child_hot, fine_counts, precision=HIGH)
    share = middle_dp // groups
    offset = clus_index * share
    middle_sums, middle_counts = (
        lax.psum_scatter(middle_part, "clus", scatter_dimension=0, tiled=True),
        lax.psum_scatter(middle_tally, "clus", scatter_dimension=0, tiled=True),
    )
    own_parent2 = lax.dynamic_slice_in_dim(parent2, offset, share, 0)
    third_share = third // devices
    third_start = (dp_index * groups + clus_index) * third_share
    third_hot = (jnp.arange(third)[:, None] == own_parent2[None, :]).astype(jnp.float32)
    third_part = jnp.dot(third_hot, middle_sums, precision=HIGH)
    third_tally = jnp.dot(third_hot, middle_counts, precision=HIGH)
    third_sums, third_counts = lax.psum((third_part, third_tally), ("dp", "clus"))
    top_hot = (jnp.arange(K4)[:, None] == parent3[None, :]).astype(jnp.float32)
    top_sums = jnp.dot(top_hot, third_sums, precision=HIGH)
    top_counts = jnp.dot(top_hot, third_counts, precision=HIGH)
    center = jnp.sum(top_sums, axis=0) / total
    top_means = shrunk(top_sums, top_counts, center[None, :], weight_top)
    third_means = shrunk(
        third_sums, third_counts, jnp.dot(top_hot.T, top_means, precision=HIGH), weight_third
    )
    third_out = lax.dynamic_slice_in_dim(third_means, third_start, third_share, 0)
    parent_hot = (own_parent2[:, None] == jnp.arange(third)[None, :]).astype(jnp.float32)
    middle_out = shrunk(
        middle_sums, middle_counts, jnp.dot(parent_hot, third_means, precision=HIGH), weight_middle
    )
    middle_means = lax.all_gather(middle_out, "clus", axis=0, tiled=True)
    fine_means = shrunk(
        fine_sums, fine_counts, jnp.dot(child_hot.T, middle_means, precision=HIGH), weight_fine
    )
    fine_out = fine_means.astype(jnp.bfloat16)
    back = jnp.dot(member, fine_out, preferred_element_type=jnp.float32)
    diff = got_rows.astype(jnp.float32) - back
    row_error = jnp.sum(diff * diff, axis=1)
    spread = jnp.sum(member.astype(jnp.float32) * row_error[:, None], axis=0) / (
        width * (fine_counts + 1.0)
    )
    return (fine_out, middle_out.astype(jnp.bfloat16), third_out.astype(jnp.bfloat16), spread)


LANES = 128
BF = jnp.bfloat16
F32 = jnp.float32
MESH = pl.DeviceIdType.MESH


def rows_hot(size, ids):
    shape = (size, ids.shape[1])
    return jnp.where(lax.broadcasted_iota(jnp.int32, shape, 0) == ids, 1.0, 0.0).astype(BF)


def column_of(ids):
    return jnp.broadcast_to(ids.astype(F32), (LANES, ids.shape[1])).T


def lanes_hot(column, start):
    lane = lax.broadcasted_iota(jnp.int32, column.shape, 1).astype(F32) + float(start)
    return jnp.where(column == lane, 1.0, 0.0).astype(BF)


def dot(a, b):
    return jnp.dot(a, b, preferred_element_type=F32)


def pieces(x, count):
    out = []
    for _ in range(count):
        part = x.astype(BF)
        out.append(part)
        x = x - part.astype(F32)
    return out


def dot_left(x, hot, count=3):
    return sum(dot(part, hot) for part in pieces(x, count))


def sweep(
    n,
    m,
    fa_ref,
    p1_ref,
    p2_ref,
    p3_ref,
    shrink_ref,
    rows_ref,
    fine_ref,
    mid_ref,
    coarse_ref,
    spread_ref,
    fa_all,
    p1_all,
    got,
    h1f,
    h2f,
    h3f,
    h1r,
    h1m,
    h23,
    base1,
    base2,
    pull1,
    pull2,
    part_own,
    pair_got,
    pair_sum,
    part_all,
    cnt_own,
    cnt_all,
    means3,
    fine_own,
    mid_own,
    coarse_own,
    err_own,
    err_all,
    tally,
    id_send,
    id_recv,
    row_send,
    row_recv,
    pair_send,
    pair_recv,
    part_send,
    part_recv,
    cnt_send,
    cnt_recv,
    back_send,
    back_recv,
    relay_send,
    relay_recv,
    fine_send,
    fine_recv,
    out_send,
    out_recv,
    local_sem,
):
    me = lax.axis_index("clus")
    dp = lax.axis_index("dp")
    count, width = rows_ref.shape
    share = width // n
    chunks = share // LANES
    fine_dev = p1_ref.shape[1]
    middle = p2_ref.shape[1]
    third = p3_ref.shape[1]
    devices = n * m
    total = count * devices
    fine = n * fine_dev
    pairs = m // 2
    half = LANES // 2
    thin = half // pairs
    pair = dp // 2
    side = lax.rem(dp, 2)
    mid_share = middle // n
    third_share = third // devices
    w4 = shrink_ref[0] * (total / K4)
    w3 = shrink_ref[1] * (total / third)
    w2 = shrink_ref[2] * (total / (middle * m))
    w1 = shrink_ref[3] * (total / (fine_dev * devices))

    def span(index, size):
        return pl.ds(pl.multiple_of(index * size, size), size)

    def chunk_of(h):
        return slice(h * LANES, (h + 1) * LANES)

    def remote(src, dst, send, recv, device):
        return pltpu.make_async_remote_copy(
            src_ref=src,
            dst_ref=dst,
            send_sem=send,
            recv_sem=recv,
            device_id=device,
            device_id_type=MESH,
        )

    def clus_peer(k):
        return {"clus": lax.rem(me + k, n)}

    def dp_peer(k):
        return {"dp": lax.rem(dp + k, m)}

    def pair_peer(k):
        return {"dp": lax.rem(pair + k, pairs) * 2 + side}

    other = {"dp": pair * 2 + 1 - side}

    started = []

    def start(copies):
        for copy in copies:
            copy.start()
        started.extend(copies)
        return copies

    def arrive(copies):
        for copy in copies:
            copy.wait_recv()

    barrier = pltpu.get_barrier_semaphore()
    for k in range(1, n):
        pl.semaphore_signal(barrier, inc=1, device_id=clus_peer(k), device_id_type=MESH)
    for k in range(1, m):
        pl.semaphore_signal(barrier, inc=1, device_id=dp_peer(k), device_id_type=MESH)
    own_rows = pltpu.make_async_copy(
        rows_ref.at[:, span(me, share)], got.at[span(me, count), :], local_sem.at[0]
    )
    own_rows.start()
    fa_all[me] = fa_ref[...]
    p1_all[me] = p1_ref[...]
    p2_row = p2_ref[...]
    p3_row = p3_ref[...]
    pl.semaphore_wait(barrier, n - 1 + m - 1)

    id_copies = []
    for k in range(1, n):
        for which, (src, dst) in enumerate(((fa_ref, fa_all), (p1_ref, p1_all))):
            id_copies.append(
                remote(src, dst.at[me], id_send.at[which, k], id_recv.at[which, k], clus_peer(k))
            )
    start(id_copies)
    row_copies = []
    for h in range(chunks):
        copies = []
        for k in range(1, n):
            column = lax.rem(me + k, n) * share + h * LANES
            copies.append(
                remote(
                    rows_ref.at[:, pl.ds(pl.multiple_of(column, LANES), LANES)],
                    got.at[span(me, count), chunk_of(h)],
                    row_send.at[h, k],
                    row_recv.at[h, k],
                    clus_peer(k),
                )
            )
        row_copies.append(start(copies))

    h23[...] = rows_hot(third, p2_row)
    h4 = lanes_hot(column_of(p3_row), 0)
    h4f = rows_hot(LANES, p3_row)
    high = p2_row // 256
    top_line = lax.broadcasted_iota(jnp.int32, (16, middle), 0) == 0
    p2_split = jnp.where(top_line, high, p2_row - high * 256).astype(F32).astype(BF)

    arrive(id_copies)
    fa_row = jnp.concatenate([fa_all[i] for i in range(n)], axis=1) - dp * fine
    p1_row = jnp.concatenate([p1_all[i] for i in range(n)], axis=1) - dp * middle
    h1f[...] = rows_hot(fine, fa_row)
    p1_lines = jnp.broadcast_to(p1_row, (16, fine)).astype(F32).astype(BF)
    mid_row = dot(p1_lines, h1f[...])[0:1].astype(jnp.int32)
    h2f[...] = rows_hot(middle, mid_row)
    halves = dot(p2_split, h2f[...])
    third_row = (halves[0:1] * 256.0 + halves[1:2]).astype(jnp.int32)
    h3f[...] = rows_hot(third, third_row)
    ones = jnp.ones((n * count, LANES), BF)
    own_rows.wait()

    pair_copies = []
    part_copies = []
    back_copies = []
    relay_copies = []
    cnt_copies = []

    def sum_part(h):
        arrive(row_copies[h])
        part_own[h] = dot(h3f[...], got[:, chunk_of(h)]).T
        away = part_own.at[h, span(1 - side, half), :]
        copy = remote(away, pair_got.at[h], pair_send.at[h], pair_recv.at[h], other)
        pair_copies.append(start([copy]))

    def sum_pair(h):
        arrive(pair_copies[h])
        pair_sum[h] = part_own[h, span(side, half), :] + pair_got[h]
        copies = []
        for k in range(1, pairs):
            copies.append(
                remote(
                    pair_sum.at[h, span(lax.rem(pair + k, pairs), thin), :],
                    part_all.at[h, pair],
                    part_send.at[h, k],
                    part_recv.at[h, k],
                    pair_peer(k),
                )
            )
        part_copies.append(start(copies))
        part_all[h, pair] = pair_sum[h, span(pair, thin), :]

    def third_level(h, cnt3, cnt4):
        arrive(part_copies[h])
        sums3 = part_all[h, 0]
        for i in range(1, pairs):
            sums3 = sums3 + part_all[h, i]
        sums4 = dot_left(sums3, h4)
        center = jnp.sum(sums4, axis=1, keepdims=True) / total
        means4 = (sums4 + w4 * center) / (cnt4 + w4)
        place = span(side * pairs + pair, thin)
        means3[h, place, :] = ((sums3 + w3 * dot_left(means4, h4f)) / (cnt3 + w3)).astype(BF)
        copies = []
        for k in range(1, pairs):
            block = means3.at[h, place, :]
            copies.append(remote(block, block, back_send.at[h, k], back_recv.at[h, k], pair_peer(k)))
        back_copies.append(start(copies))

    def relay(h):
        arrive(back_copies[h])
        block = means3.at[h, span(side, half), :]
        copy = remote(block, block, relay_send.at[h], relay_recv.at[h], other)
        relay_copies.append(start([copy]))

    sum_part(0)
    cnt_part = dot(h3f[...], ones).T[0:1]
    cnt_own[...] = cnt_part
    cnt_all[dp] = cnt_part
    for k in range(1, m):
        cnt_copies.append(
            remote(cnt_own, cnt_all.at[dp], cnt_send.at[k], cnt_recv.at[k], dp_peer(k))
        )
    start(cnt_copies)
    p1_column = column_of(p1_row)
    for j in range(0, middle, LANES):
        h1m[:, j : j + LANES] = lanes_hot(p1_column, j)
    for h in range(1, chunks):
        sum_pair(h - 1)
        sum_part(h)
    scale1 = 1.0 / (dot(h1f[...], ones) + w1)
    scale2 = 1.0 / (dot(h2f[...], ones) + w2)
    pull1[...] = w1 * scale1
    pull2[...] = w2 * scale2
    sum_pair(chunks - 1)
    for h in range(chunks):
        base1[:, chunk_of(h)] = dot(h1f[...], got[:, chunk_of(h)]) * scale1
        base2[:, chunk_of(h)] = dot(h2f[...], got[:, chunk_of(h)]) * scale2
    arrive(cnt_copies)
    cnt3 = cnt_all[0]
    for i in range(1, m):
        cnt3 = cnt3 + cnt_all[i]
    cnt4 = dot_left(jnp.broadcast_to(cnt3, (16, third)), h4)[0:1]
    for h in range(chunks):
        third_level(h, cnt3, cnt4)
    fa_column = column_of(fa_row)
    for j in range(0, fine, LANES):
        h1r[:, j : j + LANES] = lanes_hot(fa_column, j)
    fine_copies = []
    local_copies = []
    for h in range(chunks):
        relay(h)
        arrive(relay_copies[h])
        columns = pl.ds(pl.multiple_of(me * share + h * LANES, LANES), LANES)
        means2 = base2[:, chunk_of(h)] + pull2[...] * dot(means3[h], h23[...]).T
        mid_own[:, chunk_of(h)] = means2.astype(BF)
        parts = pieces(means2, 2)
        for k in (*range(1, n), 0):
            block = span(lax.rem(me + k, n), fine_dev)
            prior = sum(dot(h1m[block, :], part) for part in parts)
            means1 = base1[block, chunk_of(h)] + pull1[block, :] * prior
            fine_own[block, chunk_of(h)] = means1.astype(BF)
            src = fine_own.at[block, chunk_of(h)]
            dst = fine_ref.at[:, columns]
            if k:
                copy = remote(src, dst, fine_send.at[h, k], fine_recv.at[h, k], clus_peer(k))
                fine_copies.extend(start([copy]))
            else:
                copy = pltpu.make_async_copy(src, dst, local_sem.at[3 + h])
                copy.start()
                local_copies.append(copy)
    for h in range(chunks):
        coarse_own[:, chunk_of(h)] = means3[h].astype(F32).T.astype(BF)
    columns = span(me, share)
    out_copies = []
    plan = (
        (mid_own, mid_ref, lambda peer: span(peer, mid_share)),
        (coarse_own, coarse_ref, lambda peer: span(dp * n + peer, third_share)),
    )
    for which, (src, dst, place) in enumerate(plan):
        for k in range(1, n):
            out_copies.append(
                remote(
                    src.at[place(lax.rem(me + k, n)), :],
                    dst.at[:, columns],
                    out_send.at[which, k],
                    out_recv.at[which, k],
                    clus_peer(k),
                )
            )
        copy = pltpu.make_async_copy(
            src.at[place(me), :], dst.at[:, columns], local_sem.at[1 + which]
        )
        copy.start()
        local_copies.append(copy)
    start(out_copies)

    diff = got[...].astype(F32) - dot(h1r[...], fine_own[...])
    square = diff * diff
    folded = square[:, :LANES]
    for j in range(LANES, share, LANES):
        folded = folded + square[:, j : j + LANES]
    err_row = jnp.sum(folded.T, axis=0, keepdims=True)
    parts = pieces(err_row, 3)
    line = lax.broadcasted_iota(jnp.int32, (16, n * count), 0)
    stack = jnp.where(line == 3, 1.0, 0.0)
    for i, part in enumerate(parts):
        stack = jnp.where(line == i, part.astype(F32), stack)
    by_fine = dot(stack.astype(BF), h1r[...])
    err_fine = by_fine[0:1] + by_fine[1:2] + by_fine[2:3]
    for i in range(n):
        err_own[i] = err_fine[:, i * fine_dev : (i + 1) * fine_dev]
        tally[i] = by_fine[3:4, i * fine_dev : (i + 1) * fine_dev]
    err_copies = []
    for k in range(1, n):
        src = err_own.at[lax.rem(me + k, n)]
        err_copies.append(
            remote(src, err_all.at[me], out_send.at[2, k], out_recv.at[2, k], clus_peer(k))
        )
    start(err_copies)
    err_all[me] = err_own[me]
    arrive(err_copies)
    err = err_all[0]
    for i in range(1, n):
        err = err + err_all[i]
    spread_ref[...] = err / (width * (tally[me] + 1.0))
    for copy in local_copies:
        copy.wait()
    arrive(out_copies)
    arrive(fine_copies)
    for copy in started:
        copy.wait_send()


def land(count, *refs):
    sem = refs[-1]
    pairs = zip(refs[:count], refs[count : 2 * count])
    copies = [pltpu.make_async_copy(a, b, sem.at[i]) for i, (a, b) in enumerate(pairs)]
    for copy in copies:
        copy.start()
    for copy in copies:
        copy.wait()


def settle(*arrays):
    count = len(arrays)
    return pl.pallas_call(
        functools.partial(land, count),
        out_shape=tuple(jax.ShapeDtypeStruct(a.shape, a.dtype) for a in arrays),
        in_specs=[pl.BlockSpec(memory_space=pltpu.VMEM)] * count,
        out_specs=tuple([pl.BlockSpec(memory_space=pl.ANY)] * count),
        scratch_shapes=[pltpu.SemaphoreType.DMA((count,))],
        compiler_params=pltpu.CompilerParams(vmem_limit_bytes=4 << 20),
        name="settle",
    )(*arrays)


def fused(rows, fine_assign, parent1, parent2, parent3, shrink):
    n = lax.axis_size("clus")
    m = lax.axis_size("dp")
    count, width = rows.shape
    fine_dev = parent1.shape[0]
    middle = parent2.shape[0]
    third = parent3.shape[0]
    share = width // n
    chunks = share // LANES
    pairs = m // 2
    half = LANES // 2
    thin = half // pairs
    fine = n * fine_dev
    total_rows = n * count
    vmem = pl.BlockSpec(memory_space=pltpu.VMEM)
    dma = pltpu.SemaphoreType.DMA
    fine_out, mid_out, coarse_out, spread = pl.pallas_call(
        functools.partial(sweep, n, m),
        out_shape=(
            jax.ShapeDtypeStruct((fine_dev, width), BF),
            jax.ShapeDtypeStruct((middle // n, width), BF),
            jax.ShapeDtypeStruct((third // (n * m), width), BF),
            jax.ShapeDtypeStruct((1, fine_dev), F32),
        ),
        in_specs=[vmem] * 4
        + [pl.BlockSpec(memory_space=pltpu.SMEM), pl.BlockSpec(memory_space=pltpu.HBM)],
        out_specs=[vmem] * 4,
        scratch_shapes=[
            pltpu.VMEM((n, 1, count), jnp.int32),
            pltpu.VMEM((n, 1, fine_dev), jnp.int32),
            pltpu.VMEM((total_rows, share), BF),
            pltpu.VMEM((fine, total_rows), BF),
            pltpu.VMEM((middle, total_rows), BF),
            pltpu.VMEM((third, total_rows), BF),
            pltpu.VMEM((total_rows, fine), BF),
            pltpu.VMEM((fine, middle), BF),
            pltpu.VMEM((third, middle), BF),
            pltpu.VMEM((fine, share), F32),
            pltpu.VMEM((middle, share), F32),
            pltpu.VMEM((fine, LANES), F32),
            pltpu.VMEM((middle, LANES), F32),
            pltpu.VMEM((chunks, LANES, third), F32),
            pltpu.VMEM((chunks, half, third), F32),
            pltpu.VMEM((chunks, half, third), F32),
            pltpu.VMEM((chunks, pairs, thin, third), F32),
            pltpu.VMEM((1, third), F32),
            pltpu.VMEM((m, 1, third), F32),
            pltpu.VMEM((chunks, LANES, third), BF),
            pltpu.VMEM((fine, share), BF),
            pltpu.VMEM((middle, share), BF),
            pltpu.VMEM((third, share), BF),
            pltpu.VMEM((n, 1, fine_dev), F32),
            pltpu.VMEM((n, 1, fine_dev), F32),
            pltpu.VMEM((n, 1, fine_dev), F32),
            dma((2, n)),
            dma((2, n)),
            dma((chunks, n)),
            dma((chunks, n)),
            dma((chunks,)),
            dma((chunks,)),
            dma((chunks, pairs)),
            dma((chunks, pairs)),
            dma((m,)),
            dma((m,)),
            dma((chunks, pairs)),
            dma((chunks, pairs)),
            dma((chunks,)),
            dma((chunks,)),
            dma((chunks, n)),
            dma((chunks, n)),
            dma((3, n)),
            dma((3, n)),
            dma((3 + chunks,)),
        ],
        compiler_params=pltpu.CompilerParams(
            collective_id=0, has_side_effects=True, vmem_limit_bytes=32 << 20
        ),
        name="sweep",
    )(
        fine_assign.reshape(1, count),
        parent1.reshape(1, fine_dev),
        parent2.reshape(1, middle),
        parent3.reshape(1, third),
        shrink,
        pltpu.with_memory_space_constraint(rows, pltpu.HBM),
    )
    fine_out, mid_out, coarse_out, spread = settle(fine_out, mid_out, coarse_out, spread)
    return fine_out, mid_out, coarse_out, spread.reshape(fine_dev)


def fits(rows, fine_assign, parent1, parent2, parent3):
    n = lax.axis_size("clus")
    m = lax.axis_size("dp")
    return (
        rows.shape[1] % (n * LANES) == 0
        and m % 2 == 0
        and (LANES // 2) % (m // 2 * 16) == 0
        and rows.shape[0] % LANES == 0
        and parent1.shape[0] % LANES == 0
        and parent2.shape[0] % LANES == 0
        and parent2.shape[0] <= 256
        and parent2.shape[0] % (n * 16) == 0
        and parent3.shape[0] % LANES == 0
        and parent3.shape[0] % (n * m * 16) == 0
    )


def step(rows, fine_assign, parent1, parent2, parent3, shrink):
    form = fused if fits(rows, fine_assign, parent1, parent2, parent3) else local
    return form(rows, fine_assign, parent1, parent2, parent3, shrink)


def solution(mesh):
    placed = (P(("dp", "clus"), None), P(("dp", "clus")), P(("dp", "clus")), P("dp"), P(), P())
    return jax.shard_map(
        step,
        mesh=mesh,
        in_specs=placed,
        out_specs=(
            P(("dp", "clus"), None),
            P(("dp", "clus"), None),
            P(("dp", "clus"), None),
            P(("dp", "clus")),
        ),
        check_vma=False,
    )
```

profile of v0, /device:TPU:0, one launch (start us, length us, event | category | flops | bytes accessed | tf_op | source)
XLA Modules:
  0.0 37.5 jit_solution(11077513373068928068)
XLA Ops:
  0.6 0.0 copy-start.2
  0.6 0.0 copy-start.3
  0.7 0.0 copy-start
  0.7 0.0 copy-start.1
  0.7 0.0 copy-start.4
  0.7 0.6 %copy-done.2 = s32[256]{0:T(256)S(1)} copy-done((s32[256]{0:T(256)S(1)}, s32[256]{0:T(256)}, u32[]{:S(2)}) %copy-start.2) | copy-done | bytes 1048
  1.3 0.0 copy-done.3
  1.3 0.0 copy-done
  1.3 0.0 copy-done.1
  1.4 0.0 copy-done.4
  1.4 35.3 %sweep.1 = (bf16[256,1024]{1,0:T(8,128)(2,1)S(1)}, bf16[64,1024]{1,0:T(8,128)(2,1)S(1)}, bf16[16,1024]{1,0:T(8,128)(2,1)S(1)}, f32[1,256]{1,0:T(1,128)S(1)}) custom-call(s32[1,256]{1,0:T(1,128)S(1)} %bitcast.6, s32[1,256]{1,0:T(1,128)S(1)} %bitcast.7, s32[1,256]{1,0:T(1,128)S(1)} %bitcast.8, s32[1,512]{1,0:T(1,128)S(1)} %bitcast.5, f32[4]{0:T(128)S(1)} %copy-done.4, ...), custom_call_target="tpu_custom_call" | custom-call | tf_op jit(solution)/shard_map/sweep/pallas_call | solution.py:535
  36.7 0.9 %settle.1 = (bf16[256,1024]{1,0:T(8,128)(2,1)}, bf16[64,1024]{1,0:T(8,128)(2,1)}, bf16[16,1024]{1,0:T(8,128)(2,1)}, f32[1,256]{1,0:T(1,128)}) custom-call(bf16[256,1024]{1,0:T(8,128)(2,1)S(1)} %get-tuple-element.12.refs_0_, bf16[64,1024]{1,0:T(8,128)(2,1)S(1)} %get-tuple-element.13.refs_1_, bf16[16,1024]{1,0:T(8,128)(2,1)S(1)} %get-tuple-element.14.refs_2_, ...), custom_call_target="tpu_custom_call" | custom-call | tf_op jit(solution)/shard_map/settle/pallas_call | solution.py:508
Async XLA Ops:
  0.6 0.7 %copy-start.2 = (s32[256]{0:T(256)S(1)}, s32[256]{0:T(256)}, u32[]{:S(2)}) copy-start(s32[256]{0:T(256)} %param.8) | copy-start | bytes 3076
  0.6 0.7 %copy-start.3 = (s32[256]{0:T(256)S(1)}, s32[256]{0:T(256)}, u32[]{:S(2)}) copy-start(s32[256]{0:T(256)} %param.9) | copy-start | bytes 3076
  0.7 0.7 %copy-start = (s32[512]{0:T(512)S(1)}, s32[512]{0:T(512)}, u32[]{:S(2)}) copy-start(s32[512]{0:T(512)} %param.10) | copy-start | bytes 6148
  0.7 0.7 %copy-start.1 = (s32[256]{0:T(256)S(1)}, s32[256]{0:T(256)}, u32[]{:S(2)}) copy-start(s32[256]{0:T(256)} %param.7) | copy-start | bytes 3076
  0.7 0.7 %copy-start.4 = (f32[4]{0:T(128)S(1)}, f32[4]{0:T(128)}, u32[]{:S(2)}) copy-start(f32[4]{0:T(128)} %shrink_ref.1) | copy-start | bytes 52
where the time goes:
time: 37.7 us; the launch traced here: 37.5 us
  Pallas kernels  36.2 us (96%)
  local copies, waits for them, and re-layouts  0.69 us (2%)
  between operations  0.68 us (2%)
    pallas_call x1, Pallas kernels, fused(): pl.pallas_call(functools.partial(sweep, n, m), out_shape=(jax.ShapeDtypeS...  35.3 us
    pallas_call x1, Pallas kernels, settle(): pl.pallas_call(functools.partial(land, count), out_shape=tuple((jax.Shape...  0.87 us

commit v1 on v0

v1 whole, which is shorter than its diff:
```python
import functools

import jax
import jax.numpy as jnp
from jax import lax
from jax.experimental import pallas as pl
from jax.experimental.pallas import tpu as pltpu
from jax.sharding import PartitionSpec as P

K4 = 64


HIGH = lax.Precision.HIGHEST


def shrunk(sums, counts, prior, weight):
    return (sums + weight * prior) / (counts + weight)[:, None]


def local(rows, fine_assign, parent1, parent2, parent3, shrink):
    groups = lax.axis_size("clus")
    dp_count = lax.axis_size("dp")
    devices = groups * dp_count
    clus_index = lax.axis_index("clus")
    dp_index = lax.axis_index("dp")
    count = rows.shape[0]
    width = rows.shape[1]
    fine_dev = parent1.shape[0]
    middle_dp = parent2.shape[0]
    third = parent3.shape[0]
    slots = 2 * count // groups
    total = count * devices
    weight_top = shrink[0] * (total / K4)
    weight_third = shrink[1] * (total / third)
    weight_middle = shrink[2] * (total / (middle_dp * dp_count))
    weight_fine = shrink[3] * (total / (fine_dev * devices))
    local_ids = fine_assign - dp_index * groups * fine_dev
    target = local_ids // fine_dev
    within = local_ids - target * fine_dev
    target_hot = (target[:, None] == jnp.arange(groups)[None, :]).astype(jnp.bfloat16)
    earlier = (jnp.arange(count)[:, None] > jnp.arange(count)[None, :]).astype(jnp.bfloat16)
    before = jnp.dot(earlier, target_hot, preferred_element_type=jnp.float32)
    rank = jnp.sum(before * target_hot.astype(jnp.float32), axis=1).astype(jnp.int32)
    slot_of = target * slots + rank
    source = (
        jnp.full((groups * slots,), count, jnp.int32)
        .at[slot_of]
        .set(jnp.arange(count, dtype=jnp.int32))
    )
    padded = jnp.concatenate([rows, jnp.zeros((1, width), jnp.bfloat16)], axis=0)
    send_rows = padded[source].reshape(groups, slots, width)
    send_ids = jnp.concatenate([within, jnp.full((1,), -1, jnp.int32)])[source].reshape(
        groups, slots
    )
    got_rows, got_ids = (
        lax.all_to_all(send_rows, "clus", split_axis=0, concat_axis=0, tiled=True),
        lax.all_to_all(send_ids, "clus", split_axis=0, concat_axis=0, tiled=True),
    )
    got_rows = got_rows.reshape(groups * slots, width)
    got_ids = got_ids.reshape(groups * slots)
    member = (got_ids[:, None] == jnp.arange(fine_dev)[None, :]).astype(jnp.bfloat16)
    contract = (((0,), (0,)), ((), ()))
    fine_sums = lax.dot_general(member, got_rows, contract, preferred_element_type=jnp.float32)
    fine_counts = jnp.sum(member.astype(jnp.float32), axis=0)
    middle_local = parent1 - dp_index * middle_dp
    child_hot = (jnp.arange(middle_dp)[:, None] == middle_local[None, :]).astype(jnp.float32)
    middle_part = jnp.dot(child_hot, fine_sums, precision=HIGH)
    middle_tally = jnp.dot(child_hot, fine_counts, precision=HIGH)
    share = middle_dp // groups
    offset = clus_index * share
    middle_sums, middle_counts = (
        lax.psum_scatter(middle_part, "clus", scatter_dimension=0, tiled=True),
        lax.psum_scatter(middle_tally, "clus", scatter_dimension=0, tiled=True),
    )
    own_parent2 = lax.dynamic_slice_in_dim(parent2, offset, share, 0)
    third_share = third // devices
    third_start = (dp_index * groups + clus_index) * third_share
    third_hot = (jnp.arange(third)[:, None] == own_parent2[None, :]).astype(jnp.float32)
    third_part = jnp.dot(third_hot, middle_sums, precision=HIGH)
    third_tally = jnp.dot(third_hot, middle_counts, precision=HIGH)
    third_sums, third_counts = lax.psum((third_part, third_tally), ("dp", "clus"))
    top_hot = (jnp.arange(K4)[:, None] == parent3[None, :]).astype(jnp.float32)
    top_sums = jnp.dot(top_hot, third_sums, precision=HIGH)
    top_counts = jnp.dot(top_hot, third_counts, precision=HIGH)
    center = jnp.sum(top_sums, axis=0) / total
    top_means = shrunk(top_sums, top_counts, center[None, :], weight_top)
    third_means = shrunk(
        third_sums, third_counts, jnp.dot(top_hot.T, top_means, precision=HIGH), weight_third
    )
    third_out = lax.dynamic_slice_in_dim(third_means, third_start, third_share, 0)
    parent_hot = (own_parent2[:, None] == jnp.arange(third)[None, :]).astype(jnp.float32)
    middle_out = shrunk(
        middle_sums, middle_counts, jnp.dot(parent_hot, third_means, precision=HIGH), weight_middle
    )
    middle_means = lax.all_gather(middle_out, "clus", axis=0, tiled=True)
    fine_means = shrunk(
        fine_sums, fine_counts, jnp.dot(child_hot.T, middle_means, precision=HIGH), weight_fine
    )
    fine_out = fine_means.astype(jnp.bfloat16)
    back = jnp.dot(member, fine_out, preferred_element_type=jnp.float32)
    diff = got_rows.astype(jnp.float32) - back
    row_error = jnp.sum(diff * diff, axis=1)
    spread = jnp.sum(member.astype(jnp.float32) * row_error[:, None], axis=0) / (
        width * (fine_counts + 1.0)
    )
    return (fine_out, middle_out.astype(jnp.bfloat16), third_out.astype(jnp.bfloat16), spread)


LANES = 128
HALF = LANES // 2
BF = jnp.bfloat16
F32 = jnp.float32
MESH = pl.DeviceIdType.MESH


def rows_hot(size, ids):
    shape = (size, ids.shape[1])
    return jnp.where(lax.broadcasted_iota(jnp.int32, shape, 0) == ids, 1.0, 0.0).astype(BF)


def column_of(ids):
    return jnp.broadcast_to(ids.astype(F32), (LANES, ids.shape[1])).T


def lanes_hot(column, start):
    lane = lax.broadcasted_iota(jnp.int32, column.shape, 1).astype(F32) + float(start)
    return jnp.where(column == lane, 1.0, 0.0).astype(BF)


def dot(a, b):
    return jnp.dot(a, b, preferred_element_type=F32)


def pieces(x, count):
    out = []
    for _ in range(count):
        part = x.astype(BF)
        out.append(part)
        x = x - part.astype(F32)
    return out


def dot_left(x, hot, count=3):
    return sum(dot(part, hot) for part in pieces(x, count))


def halves(a, b, part):
    lane = slice(part * HALF, (part + 1) * HALF)
    return jnp.concatenate([a[:, lane], b[:, lane]], axis=1)


def dot_stack(x, hot):
    both = dot(jnp.concatenate(pieces(x, 2), axis=0), hot)
    return both[: x.shape[0]] + both[x.shape[0] :]


def sweep(
    n,
    m,
    fa_hbm,
    p1_hbm,
    p2_hbm,
    p3_hbm,
    shrink_hbm,
    rows_ref,
    fine_ref,
    mid_ref,
    coarse_ref,
    spread_ref,
    fa_all,
    p1_all,
    p2_all,
    p3_ref,
    shrink_ref,
    rows_own,
    row_out,
    row_in,
    got,
    h1f,
    h2f,
    h1r,
    h1m,
    ht,
    hn,
    sums2,
    base1,
    pull1,
    scale2,
    rate1,
    part_own,
    part_all,
    cnt_own,
    cnt_all,
    cnt_third,
    cnt_top,
    means3,
    back_own,
    back_all,
    coarse_all,
    mid_half,
    fine_out,
    fine_in,
    fine_own,
    mid_own,
    coarse_own,
    err_own,
    err_all,
    tally,
    in_sem,
    id_send,
    id_recv,
    p2_send,
    p2_recv,
    row_send,
    row_recv,
    part_send,
    part_recv,
    cnt_send,
    cnt_recv,
    back_send,
    back_recv,
    fine_send,
    fine_recv,
    mid_send,
    mid_recv,
    out_send,
    out_recv,
    err_send,
    err_recv,
    local_sem,
):
    me = lax.axis_index("clus")
    dp = lax.axis_index("dp")
    count, width = rows_ref.shape
    share = width // n
    tiles = share // LANES
    chunks = 2 * tiles
    fine_dev = p1_hbm.shape[1]
    middle = p2_hbm.shape[1]
    third = p3_hbm.shape[1]
    devices = n * m
    total = count * devices
    fine = n * fine_dev
    some = count // 2
    few = fine_dev // 2
    packed = n * some
    center_dp = m // 2 // 2 * 2
    pairs = m // 2
    pair = dp // 2
    side = lax.rem(dp, 2)
    near = (center_dp // 2 - 1, center_dp // 2)
    far = (0, pairs - 1)
    plan = [far if q == 2 else near for q in range(chunks)]
    size = 4
    thin = HALF // size
    window = third // pairs
    mid_share = middle // n
    third_share = third // devices

    def span(index, size):
        return pl.ds(pl.multiple_of(index * size, size), size)

    def tile_of(t):
        return slice(t * LANES, (t + 1) * LANES)

    def column(index, t):
        return pl.ds(pl.multiple_of(index * share + t * LANES, LANES), LANES)

    def remote(src, dst, send, recv, device):
        return pltpu.make_async_remote_copy(
            src_ref=src,
            dst_ref=dst,
            send_sem=send,
            recv_sem=recv,
            device_id=device,
            device_id_type=MESH,
        )

    if n == 4:
        peers = [n - 1 - me, lax.rem(me + 2, n), me + 1 - 2 * lax.rem(me, 2)]
    else:
        peers = [lax.rem(me + k, n) for k in range(1, n)]

    def dp_peer(k):
        return lax.rem(dp + k, m)

    started = []

    def start(copies):
        for copy in copies:
            copy.start()
        started.extend(copies)
        return copies

    def arrive(copies):
        for copy in copies:
            copy.wait_recv()

    low_half = pair < pairs // 2

    def close(q):
        return jnp.where(low_half, plan[q][0], plan[q][1])

    def owners(q):
        other = jnp.where(low_half, plan[q][1], plan[q][0])
        block = jnp.where(low_half, 2, 0)
        own = 2 - block
        return (
            (other * 2, block),
            (other * 2 + 1, block + 1),
            (close(q) * 2 + 1 - side, own + 1 - side),
            (close(q) * 2 + side, own + side),
        )

    def is_owner(q):
        return pair == close(q)

    def slot(q):
        return owners(q)[3][1]

    if pairs == 4:
        inward = jnp.where(low_half, pair + 1, pair - 1)
        last = jnp.where(low_half, 3, 0)
        chips = [inward, 6 - pair - inward - last, last]
    else:
        chips = [lax.rem(pair + k, pairs) for k in range(1, pairs)]
    others = [chip * 2 + core for chip in reversed(chips) for core in range(2)]
    others.append(pair * 2 + 1 - side)

    barrier = pltpu.get_barrier_semaphore()
    for peer in peers:
        pl.semaphore_signal(barrier, inc=1, device_id={"clus": peer}, device_id_type=MESH)
    for k in range(1, m):
        pl.semaphore_signal(barrier, inc=1, device_id={"dp": dp_peer(k)}, device_id_type=MESH)
    fetch = [
        pltpu.make_async_copy(src, dst, in_sem.at[i])
        for i, (src, dst) in enumerate(
            [
                (fa_hbm, fa_all.at[me]),
                (p1_hbm, p1_all.at[me]),
                (p2_hbm, p2_all.at[dp]),
                (rows_ref, rows_own),
                (p3_hbm, p3_ref),
                (shrink_hbm, shrink_ref),
            ]
        )
    ]
    for copy in fetch:
        copy.start()
    pl.semaphore_wait(barrier, n - 1 + m - 1)
    for copy in fetch[:3]:
        copy.wait()

    id_copies = []
    for k, peer in enumerate(peers):
        for which, ids in enumerate((fa_all, p1_all)):
            own = ids.at[me]
            id_copies.append(
                remote(own, own, id_send.at[which, k], id_recv.at[which, k], {"clus": peer})
            )
    start(id_copies)
    start(
        [
            remote(
                p2_all.at[dp], p2_all.at[dp], p2_send.at[k], p2_recv.at[dp], {"dp": dp_peer(k)}
            )
            for k in range(1, m)
        ]
    )
    fetch[3].wait()
    row_copies = []
    for q in range(chunks):
        t, a = divmod(q, 2)
        for p in range(n):
            lane = slice(p * share + t * LANES, p * share + (t + 1) * LANES)
            row_out[q, p] = halves(rows_own[0:some, lane], rows_own[some:count, lane], a)
        row_copies.append(
            start(
                [
                    remote(
                        row_out.at[q, peer],
                        row_in.at[q, span(me, some), :],
                        row_send.at[q, k],
                        row_recv.at[q, k],
                        {"clus": peer},
                    )
                    for k, peer in enumerate(peers)
                ]
            )
        )
        row_in[q, span(me, some), :] = row_out[q, me]

    for copy in fetch[4:]:
        copy.wait()
    w4 = shrink_ref[0] * (total / K4)
    w3 = shrink_ref[1] * (total / third)
    w2 = shrink_ref[2] * (total / (middle * m))
    w1 = shrink_ref[3] * (total / (fine_dev * devices))
    p3_row = p3_ref[...]
    h4 = lanes_hot(column_of(p3_row), 0)
    h4f = rows_hot(LANES, p3_row)
    ones = jnp.ones((LANES, LANES), BF)

    def left_half(size):
        return lax.broadcasted_iota(jnp.int32, (size, LANES), 1) < HALF

    def parents_of(i, own):
        if not own:
            block = p2_all.at[i]
            remote(block, block, p2_send.at[0], p2_recv.at[i], {"dp": i}).wait_recv()
        row = p2_all[i]
        ht[:, span(i, middle)] = rows_hot(third, row)
        p2_column = column_of(row)
        for j in range(0, third, LANES):
            hn[span(i, middle), j : j + LANES] = lanes_hot(p2_column, j)

    parents_of(dp, True)
    parents_of(pair * 2 + 1 - side, False)
    parents_of(chips[0] * 2, False)
    parents_of(chips[0] * 2 + 1, False)
    arrive(id_copies)
    ids = [fa_all[i] for i in range(n)]
    ids = [x[:, 0:some] for x in ids] + [x[:, some:count] for x in ids]
    fa_row = jnp.concatenate(ids, axis=1) - dp * fine
    table = [
        p1_all[i][:, j : j + LANES] for i in range(n) for j in range(0, fine_dev, LANES)
    ]
    table = (jnp.concatenate(table, axis=0) - dp * middle).astype(F32).astype(BF)
    line = fa_row // LANES
    picked = dot(table, rows_hot(LANES, fa_row - line * LANES))
    lines = lax.broadcasted_iota(jnp.int32, picked.shape, 0)
    mid_row = jnp.sum(jnp.where(lines == line, picked, 0.0), axis=0, keepdims=True)
    h2f[...] = rows_hot(middle, mid_row.astype(jnp.int32))

    def part_copy(q, k):
        device, o = owners(q)[k]
        return remote(
            part_own.at[q, span(o, thin), :],
            part_all.at[q, dp],
            part_send.at[q, k],
            part_recv.at[q, dp],
            {"dp": device},
        )

    def part_from(q, i):
        block = part_all.at[q, i]
        return remote(block, block, part_send.at[q, 0], part_recv.at[q, i], {"dp": i})

    def cnt_copy(k):
        peer = dp_peer(k)
        return remote(cnt_own, cnt_all.at[dp], cnt_send.at[k], cnt_recv.at[dp], {"dp": peer})

    def cnt_from(i):
        return remote(cnt_own, cnt_all.at[i], cnt_send.at[0], cnt_recv.at[i], {"dp": i})

    def sum_part(q):
        arrive(row_copies[q])
        block = row_in[q]
        both = jnp.where(
            left_half(middle), dot(h2f[:, 0:packed], block), dot(h2f[:, packed:], block)
        )
        both = both + pltpu.roll(both, HALF, 1)
        part_own[q] = both.T[0:HALF].astype(BF)
        for k in range(size - 1):
            part_copy(q, k).start()

        @pl.when(is_owner(q))
        def _():
            part_all[q, dp] = part_own[q, span(slot(q), thin), :]

        @pl.when(jnp.logical_not(is_owner(q)))
        def _():
            part_copy(q, size - 1).start()

        sums2[q] = both

    count2 = h2f[:, 0:LANES]
    for j in range(LANES, n * count, LANES):
        count2 = count2 + h2f[:, j : j + LANES]
    count2 = dot(count2, ones)
    cnt_own[...] = count2.T[0:1]
    for k in range(1, m):
        cnt_copy(k).start()
    cnt_all[dp] = cnt_own[...]
    sum_part(0)
    for chip in chips[1:]:
        parents_of(chip * 2, False)
        parents_of(chip * 2 + 1, False)

    def back_copy(q, k):
        peer = others[k]
        return remote(
            back_own.at[q, :, span(peer, middle)],
            back_all.at[q, span(slot(q), thin), :],
            back_send.at[0, q, k],
            back_recv.at[0, q, slot(q)],
            {"dp": peer},
        )

    def coarse_copy(q, k):
        peer = others[k]
        return remote(
            means3.at[q, :, span(peer // 2, window)],
            coarse_all.at[q, span(slot(q), thin), :],
            back_send.at[1, q, k],
            back_recv.at[1, q, slot(q)],
            {"dp": peer},
        )

    def from_owners(which, q):
        dst = (back_all, coarse_all)[which]

        def wait(k):
            device, o = owners(q)[k]
            block = dst.at[q, span(o, thin), :]
            send, recv = back_send.at[which, q, 0], back_recv.at[which, q, o]
            remote(block, block, send, recv, {"dp": device}).wait_recv()

        for k in range(size - 1):
            wait(k)

        @pl.when(jnp.logical_not(is_owner(q)))
        def _():
            wait(size - 1)

    def third_level(q):
        total3 = jnp.zeros((thin + 16, third), F32)
        if q == plan.index(plan[q]):
            for i in others:
                cnt_from(i).wait_recv()
        for chip in (pair, *chips):
            for i in (chip * 2, chip * 2 + 1) if chip is not pair else (pair * 2 + 1 - side,):
                part_from(q, i).wait_recv()
            block = jnp.concatenate([part_all[q, chip * 2 + c] for c in range(2)], axis=1)
            if q == plan.index(plan[q]):
                lines = jnp.concatenate([cnt_all[chip * 2 + c] for c in range(2)], axis=1)
                row = lax.broadcasted_iota(jnp.int32, (16, 2 * middle), 0)
                stack = jnp.zeros((16, 2 * middle), F32)
                for i, part in enumerate(pieces(lines, 3)):
                    stack = jnp.where(row == i, part.astype(F32), stack)
                block = jnp.concatenate([block, stack.astype(BF)], axis=0)
                total3 = total3 + dot(block, hn[span(chip, 2 * middle), :])
            else:
                total3 = total3[0:thin] + dot(block, hn[span(chip, 2 * middle), :])
        sums3 = total3[0:thin]
        if q == plan.index(plan[q]):
            cnt3 = total3[thin : thin + 1] + total3[thin + 1 : thin + 2] + total3[thin + 2 : thin + 3]
            cnt_third[...] = cnt3
            both = jnp.concatenate([sums3, jnp.broadcast_to(cnt3, (16, third))], axis=0)
            both = dot_stack(both, h4)
            sums4, cnt4 = both[0:thin], both[thin : thin + 1]
            cnt_top[...] = cnt4
        else:
            cnt3, cnt4 = cnt_third[...], cnt_top[...]
            sums4 = dot_stack(sums3, h4)
        center = jnp.sum(sums4, axis=1, keepdims=True) / total
        means4 = (sums4 + w4 * center) / (cnt4 + w4)
        block = ((sums3 + w3 * dot_stack(means4, h4f)) / (cnt3 + w3)).astype(BF)
        means3[q] = block
        back_own[q] = dot(block, ht[...]).astype(BF)
        for k in range(m - 1):
            back_copy(q, k).start()
        for k in range(m - 1):
            coarse_copy(q, k).start()
        back_all[q, span(slot(q), thin), :] = back_own[q, :, span(dp, middle)]
        coarse_all[q, span(slot(q), thin), :] = means3[q, :, span(dp // 2, window)]

    def run_third(q):
        @pl.when(is_owner(q))
        def _():
            third_level(q)

    def unpack(t):
        a, b = row_in[2 * t], row_in[2 * t + 1]
        got[0:packed, tile_of(t)] = halves(a, b, 0)
        got[packed:, tile_of(t)] = halves(a, b, 1)

    def fine_counts():
        some_counts = h1f[:, 0:LANES]
        for j in range(LANES, n * count, LANES):
            some_counts = some_counts + h1f[:, j : j + LANES]
        return dot(some_counts, ones)

    def bases(t):
        unpack(t)
        left = left_half(few)
        if t == 0:
            scale2[...] = 1.0 / (count2 + w2)
            rate1[...] = 1.0 / (fine_counts() + w1)
        sums1 = dot(h1f[...], got[:, tile_of(t)])
        for p in range(n):
            low = slice(p * fine_dev, p * fine_dev + few)
            high = slice(p * fine_dev + few, (p + 1) * fine_dev)
            place = slice(p * few, (p + 1) * few)
            rate_a, rate_b = rate1[low], rate1[high]
            if t == 0:
                pull1[place, :] = w1 * jnp.where(left, rate_a, rate_b)
            a = sums1[low] * rate_a
            b = sums1[high] * rate_b
            base1[2 * t, place, :] = halves(a, b, 0)
            base1[2 * t + 1, place, :] = halves(a, b, 1)

    fine_copies = []
    mid_copies = []
    local_copies = []

    def down(q):
        t, a = divmod(q, 2)
        from_owners(0, q)
        prior2 = back_all[q].astype(F32)
        prior2 = jnp.concatenate([prior2, prior2], axis=0).T
        means2 = (sums2[q] + w2 * prior2) * scale2[...]
        prior1 = sum(dot(h1m[...], part) for part in pieces(means2, 2))
        left = left_half(few)
        for p in range(n):
            low = prior1[p * fine_dev : p * fine_dev + few]
            high = prior1[p * fine_dev + few : (p + 1) * fine_dev]
            place = slice(p * few, (p + 1) * few)
            means1 = base1[q, place] + pull1[place] * jnp.where(left, low, high)
            fine_out[q, p] = means1.astype(BF)
        copies = start(
            [
                remote(
                    fine_out.at[q, peer],
                    fine_in.at[q, me],
                    fine_send.at[q, k],
                    fine_recv.at[q, k],
                    {"clus": peer},
                )
                for k, peer in enumerate(peers)
            ]
        )
        fine_copies.append(copies)
        if not a:
            mid_half[...] = means2
            return
        mid_own[:, tile_of(t)] = jnp.where(left_half(middle), mid_half[...], means2).astype(BF)
        for k, peer in enumerate(peers):
            mid_copies.extend(
                start(
                    [
                        remote(
                            mid_own.at[span(peer, mid_share), tile_of(t)],
                            mid_ref.at[:, column(me, t)],
                            mid_send.at[t, k],
                            mid_recv.at[t, k],
                            {"clus": peer},
                        )
                    ]
                )
            )
        copy = pltpu.make_async_copy(
            mid_own.at[span(me, mid_share), tile_of(t)], mid_ref.at[:, column(me, t)], local_sem.at[t]
        )
        copy.start()
        local_copies.append(copy)

    def rows_by_fine():
        fa_column = column_of(fa_row)
        for j in range(0, fine, LANES):
            h1r[:, j : j + LANES] = lanes_hot(fa_column, j)

    def coarse(t):
        for q in (2 * t, 2 * t + 1):
            from_owners(1, q)
        block = jnp.concatenate([coarse_all[2 * t], coarse_all[2 * t + 1]], axis=0)
        coarse_own[:, tile_of(t)] = block.astype(F32).T.astype(BF)

        def place(peer):
            return coarse_own.at[span(side * n + peer, third_share), tile_of(t)]

        out_copies.extend(
            start(
                [
                    remote(
                        place(peer),
                        coarse_ref.at[:, column(me, t)],
                        out_send.at[t, k],
                        out_recv.at[t, k],
                        {"clus": peer},
                    )
                    for k, peer in enumerate(peers)
                ]
            )
        )
        copy = pltpu.make_async_copy(
            place(me), coarse_ref.at[:, column(me, t)], local_sem.at[tiles + t]
        )
        copy.start()
        local_copies.append(copy)

    def fine_tile(t):
        for p in range(n):
            a, b = fine_out[2 * t, p], fine_out[2 * t + 1, p]
            fine_own[p * fine_dev : p * fine_dev + few, tile_of(t)] = halves(a, b, 0)
            fine_own[p * fine_dev + few : (p + 1) * fine_dev, tile_of(t)] = halves(a, b, 1)

    out_copies = []
    p1_row = jnp.concatenate([p1_all[i] for i in range(n)], axis=1) - dp * middle
    p1_column = column_of(p1_row)
    for j in range(0, middle, LANES):
        h1m[:, j : j + LANES] = lanes_hot(p1_column, j)
    sum_part(1)
    h1f[...] = rows_hot(fine, fa_row)
    for q in range(2, chunks - 1):
        sum_part(q)
    bases(0)
    run_third(0)
    sum_part(chunks - 1)
    run_third(1)
    for t in range(1, tiles):
        bases(t)
    run_third(2)
    down(0)
    for q in range(3, chunks):
        run_third(q)
    for q in range(1, chunks):
        down(q)
        if q % 2 and q < chunks - 1:
            coarse(q // 2)
            fine_tile(q // 2)
            rows_by_fine()
    if chunks == 2:
        rows_by_fine()
    coarse(tiles - 1)
    fine_tile(tiles - 1)
    fine_ref[:, span(me, share)] = fine_own[span(me, fine_dev), :]
    diff = got[...].astype(F32) - dot(h1r[...], fine_own[...])
    square = diff * diff
    folded = square[:, :LANES]
    for j in range(LANES, share, LANES):
        folded = folded + square[:, j : j + LANES]
    square = folded
    err_row = jnp.sum(square.T, axis=0, keepdims=True)
    parts = pieces(err_row, 3)
    line = lax.broadcasted_iota(jnp.int32, (16, n * count), 0)
    stack = jnp.where(line == 3, 1.0, 0.0)
    for i, part in enumerate(parts):
        stack = jnp.where(line == i, part.astype(F32), stack)
    by_fine = dot(stack.astype(BF), h1r[...])
    err_fine = by_fine[0:1] + by_fine[1:2] + by_fine[2:3]
    for i in range(n):
        err_own[i] = err_fine[:, i * fine_dev : (i + 1) * fine_dev]
        tally[i] = by_fine[3:4, i * fine_dev : (i + 1) * fine_dev]
    err_copies = start(
        [
            remote(
                err_own.at[peer],
                err_all.at[me],
                err_send.at[k],
                err_recv.at[k],
                {"clus": peer},
            )
            for k, peer in enumerate(peers)
        ]
    )
    err_all[me] = err_own[me]

    for t in range(tiles):
        for q in (2 * t, 2 * t + 1):
            arrive(fine_copies[q])
        for k in range(1, n):
            peer = lax.rem(me + k, n)
            a, b = fine_in[2 * t, peer], fine_in[2 * t + 1, peer]
            fine_ref[0:few, column(peer, t)] = halves(a, b, 0)
            fine_ref[few:, column(peer, t)] = halves(a, b, 1)
    arrive(err_copies)
    err = err_all[0]
    for i in range(1, n):
        err = err + err_all[i]
    spread_ref[...] = err / (width * (tally[me] + 1.0))
    for copy in local_copies:
        copy.wait()
    arrive(mid_copies)
    arrive(out_copies)
    for copy in started:
        copy.wait_send()
    for k in range(1, m):
        cnt_copy(k).wait_send()
    for q in range(chunks):
        for k in range(size - 1):
            part_copy(q, k).wait_send()

    def drain(q):
        @pl.when(is_owner(q))
        def _():
            for k in range(m - 1):
                back_copy(q, k).wait_send()
                coarse_copy(q, k).wait_send()

        @pl.when(jnp.logical_not(is_owner(q)))
        def _():
            part_copy(q, size - 1).wait_send()

    for q in range(chunks):
        drain(q)


def land(count, *refs):
    sem = refs[-1]
    pairs = zip(refs[:count], refs[count : 2 * count])
    copies = [pltpu.make_async_copy(a, b, sem.at[i]) for i, (a, b) in enumerate(pairs)]
    for copy in copies:
        copy.start()
    for copy in copies:
        copy.wait()


def settle(*arrays):
    count = len(arrays)
    return pl.pallas_call(
        functools.partial(land, count),
        out_shape=tuple(jax.ShapeDtypeStruct(a.shape, a.dtype) for a in arrays),
        in_specs=[pl.BlockSpec(memory_space=pltpu.VMEM)] * count,
        out_specs=tuple([pl.BlockSpec(memory_space=pl.ANY)] * count),
        scratch_shapes=[pltpu.SemaphoreType.DMA((count,))],
        compiler_params=pltpu.CompilerParams(vmem_limit_bytes=4 << 20),
        name="settle",
    )(*arrays)


def fused(rows, fine_assign, parent1, parent2, parent3, shrink):
    n = lax.axis_size("clus")
    m = lax.axis_size("dp")
    count, width = rows.shape
    fine_dev = parent1.shape[0]
    middle = parent2.shape[0]
    third = parent3.shape[0]
    share = width // n
    tiles = share // LANES
    chunks = 2 * tiles
    window = third // (m // 2)
    fine = n * fine_dev
    total_rows = n * count
    vmem = pl.BlockSpec(memory_space=pltpu.VMEM)
    hbm = pl.BlockSpec(memory_space=pltpu.HBM)
    dma = pltpu.SemaphoreType.DMA

    def stay(x):
        return pltpu.with_memory_space_constraint(x, pltpu.HBM)

    fine_out, mid_out, coarse_out, spread = pl.pallas_call(
        functools.partial(sweep, n, m),
        out_shape=(
            jax.ShapeDtypeStruct((fine_dev, width), BF),
            jax.ShapeDtypeStruct((middle // n, width), BF),
            jax.ShapeDtypeStruct((third // (n * m), width), BF),
            jax.ShapeDtypeStruct((1, fine_dev), F32),
        ),
        in_specs=[hbm] * 6,
        out_specs=[vmem] * 4,
        scratch_shapes=[
            pltpu.VMEM((n, 1, count), jnp.int32),
            pltpu.VMEM((n, 1, fine_dev), jnp.int32),
            pltpu.VMEM((m, 1, middle), jnp.int32),
            pltpu.VMEM((1, third), jnp.int32),
            pltpu.SMEM((4,), F32),
            pltpu.VMEM((count, width), BF),
            pltpu.VMEM((chunks, n, count // 2, LANES), BF),
            pltpu.VMEM((chunks, total_rows // 2, LANES), BF),
            pltpu.VMEM((total_rows, share), BF),
            pltpu.VMEM((fine, total_rows), BF),
            pltpu.VMEM((middle, total_rows), BF),
            pltpu.VMEM((total_rows, fine), BF),
            pltpu.VMEM((fine, middle), BF),
            pltpu.VMEM((third, m * middle), BF),
            pltpu.VMEM((m * middle, third), BF),
            pltpu.VMEM((chunks, middle, LANES), F32),
            pltpu.VMEM((chunks, fine // 2, LANES), F32),
            pltpu.VMEM((fine // 2, LANES), F32),
            pltpu.VMEM((middle, LANES), F32),
            pltpu.VMEM((fine, LANES), F32),
            pltpu.VMEM((chunks, HALF, middle), BF),
            pltpu.VMEM((chunks, m, HALF // 4, middle), BF),
            pltpu.VMEM((1, middle), F32),
            pltpu.VMEM((m, 1, middle), F32),
            pltpu.VMEM((1, third), F32),
            pltpu.VMEM((1, LANES), F32),
            pltpu.VMEM((chunks, HALF // 4, third), BF),
            pltpu.VMEM((chunks, HALF // 4, m * middle), BF),
            pltpu.VMEM((chunks, HALF, middle), BF),
            pltpu.VMEM((chunks, HALF, window), BF),
            pltpu.VMEM((middle, LANES), F32),
            pltpu.VMEM((chunks, n, fine_dev // 2, LANES), BF),
            pltpu.VMEM((chunks, n, fine_dev // 2, LANES), BF),
            pltpu.VMEM((fine, share), BF),
            pltpu.VMEM((middle, share), BF),
            pltpu.VMEM((window, share), BF),
            pltpu.VMEM((n, 1, fine_dev), F32),
            pltpu.VMEM((n, 1, fine_dev), F32),
            pltpu.VMEM((n, 1, fine_dev), F32),
            dma((6,)),
            dma((2, n)),
            dma((2, n)),
            dma((m,)),
            dma((m,)),
            dma((chunks, n)),
            dma((chunks, n)),
            dma((chunks, 4)),
            dma((chunks, m)),
            dma((m,)),
            dma((m,)),
            dma((2, chunks, m)),
            dma((2, chunks, 4)),
            dma((chunks, n)),
            dma((chunks, n)),
            dma((tiles, n)),
            dma((tiles, n)),
            dma((tiles, n)),
            dma((tiles, n)),
            dma((n,)),
            dma((n,)),
            dma((2 * tiles,)),
        ],
        compiler_params=pltpu.CompilerParams(
            collective_id=0, has_side_effects=True, vmem_limit_bytes=40 << 20
        ),
        name="sweep",
    )(
        stay(fine_assign.reshape(1, count)),
        stay(parent1.reshape(1, fine_dev)),
        stay(parent2.reshape(1, middle)),
        stay(parent3.reshape(1, third)),
        stay(shrink),
        stay(rows),
    )
    fine_out, mid_out, coarse_out, spread = settle(fine_out, mid_out, coarse_out, spread)
    return fine_out, mid_out, coarse_out, spread.reshape(fine_dev)


def fits(rows, fine_assign, parent1, parent2, parent3):
    n = lax.axis_size("clus")
    m = lax.axis_size("dp")
    return (
        rows.shape[1] % (n * LANES) == 0
        and m % 2 == 0
        and m >= 4
        and rows.shape[0] % (2 * LANES) == 0
        and parent1.shape[0] % LANES == 0
        and parent2.shape[0] % LANES == 0
        and parent2.shape[0] <= 256
        and parent2.shape[0] % (n * 16) == 0
        and parent3.shape[0] % (m // 2 * LANES) == 0
        and parent3.shape[0] % (n * m * 16) == 0
    )


def step(rows, fine_assign, parent1, parent2, parent3, shrink):
    form = fused if fits(rows, fine_assign, parent1, parent2, parent3) else local
    return form(rows, fine_assign, parent1, parent2, parent3, shrink)


def solution(mesh):
    placed = (P(("dp", "clus"), None), P(("dp", "clus")), P(("dp", "clus")), P("dp"), P(), P())
    return jax.shard_map(
        step,
        mesh=mesh,
        in_specs=placed,
        out_specs=(
            P(("dp", "clus"), None),
            P(("dp", "clus"), None),
            P(("dp", "clus"), None),
            P(("dp", "clus")),
        ),
        check_vma=False,
    )
```

time: 37.7 us -> 33.4 us (0.89)
  Pallas kernels: 36.2 us -> 32.5 us
  local copies, waits for them, and re-layouts: 0.69 us -> 0 us
    pallas_call x1, Pallas kernels: 35.3 us -> 31.6 us  [fused(): pl.pallas_call(functools.partial(sweep, n, m), out_shape=(jax.ShapeDtypeS...]
    unnamed x10 -> x0, local copies, waits for them, and re-layouts: 0.69 us -> none
where the time goes in v1:
time: 33.4 us; the launch traced here: 33.3 us
  Pallas kernels  32.5 us (97%)
  between operations  0.8 us (2%)
    pallas_call x1, Pallas kernels, fused(): pl.pallas_call(functools.partial(sweep, n, m), out_shape=(jax.ShapeDtypeS...  31.6 us
    pallas_call x1, Pallas kernels, settle(): pl.pallas_call(functools.partial(land, count), out_shape=tuple((jax.Shape...  0.87 us

profile of v1, /device:TPU:0, one launch (start us, length us, event | category | flops | bytes accessed | tf_op | source)
XLA Modules:
  0.0 33.3 jit_solution(15624222603612157784)
XLA Ops:
  0.6 31.6 %sweep.1 = (bf16[256,1024]{1,0:T(8,128)(2,1)S(1)}, bf16[64,1024]{1,0:T(8,128)(2,1)S(1)}, bf16[16,1024]{1,0:T(8,128)(2,1)S(1)}, f32[1,256]{1,0:T(1,128)S(1)}) custom-call(s32[1,256]{1,0:T(1,128)} %bitcast.6, s32[1,256]{1,0:T(1,128)} %bitcast.7, s32[1,256]{1,0:T(1,128)} %bitcast.8, s32[1,512]{1,0:T(1,128)} %bitcast.5, f32[4]{0:T(128)} %shrink_hbm.1, ...), custom_call_target="tpu_custom_call" | custom-call | tf_op jit(solution)/shard_map/sweep/pallas_call | solution.py:842
  32.3 0.9 %settle.1 = (bf16[256,1024]{1,0:T(8,128)(2,1)}, bf16[64,1024]{1,0:T(8,128)(2,1)}, bf16[16,1024]{1,0:T(8,128)(2,1)}, f32[1,256]{1,0:T(1,128)}) custom-call(bf16[256,1024]{1,0:T(8,128)(2,1)S(1)} %get-tuple-element.12.refs_0_, bf16[64,1024]{1,0:T(8,128)(2,1)S(1)} %get-tuple-element.13.refs_1_, bf16[16,1024]{1,0:T(8,128)(2,1)S(1)} %get-tuple-element.14.refs_2_, ...), custom_call_target="tpu_custom_call" | custom-call | tf_op jit(solution)/shard_map/settle/pallas_call | solution.py:811

commit v2 on v1

--- a/solution.py
+++ b/solution.py
@@ -115,16 +115,20 @@
 
 def rows_hot(size, ids):
     shape = (size, ids.shape[1])
-    return jnp.where(lax.broadcasted_iota(jnp.int32, shape, 0) == ids, 1.0, 0.0).astype(BF)
+    lines = lax.broadcasted_iota(jnp.int16, shape, 0)
+    same = lines == jnp.broadcast_to(ids.astype(jnp.int16), shape)
+    return jnp.where(same, jnp.ones(shape, BF), jnp.zeros(shape, BF))
 
 
 def column_of(ids):
-    return jnp.broadcast_to(ids.astype(F32), (LANES, ids.shape[1])).T
+    column = jnp.broadcast_to(ids.astype(F32), (LANES, ids.shape[1])).T
+    return column.astype(jnp.int32).astype(jnp.int16)
 
 
 def lanes_hot(column, start):
-    lane = lax.broadcasted_iota(jnp.int32, column.shape, 1).astype(F32) + float(start)
-    return jnp.where(column == lane, 1.0, 0.0).astype(BF)
+    shape = column.shape
+    same = column == lax.broadcasted_iota(jnp.int16, shape, 1) + jnp.int16(start)
+    return jnp.where(same, jnp.ones(shape, BF), jnp.zeros(shape, BF))
 
 
 def dot(a, b):
@@ -186,7 +190,6 @@
     base1,
     pull1,
     scale2,
-    rate1,
     part_own,
     part_all,
     cnt_own,
@@ -219,6 +222,7 @@
     cnt_recv,
     back_send,
     back_recv,
+    coarse_recv,
     fine_send,
     fine_recv,
     mid_send,
@@ -249,8 +253,6 @@
     pair = dp // 2
     side = lax.rem(dp, 2)
     near = (center_dp // 2 - 1, center_dp // 2)
-    far = (0, pairs - 1)
-    plan = [far if q == 2 else near for q in range(chunks)]
     size = 4
     thin = HALF // size
     window = third // pairs
@@ -281,42 +283,38 @@
     else:
         peers = [lax.rem(me + k, n) for k in range(1, n)]
 
-    def dp_peer(k):
-        return lax.rem(dp + k, m)
-
-    started = []
-
     def start(copies):
         for copy in copies:
             copy.start()
-        started.extend(copies)
-        return copies
-
-    def arrive(copies):
-        for copy in copies:
-            copy.wait_recv()
+
+    def landed(ref, sem):
+        pltpu.make_async_copy(ref, ref, sem).wait()
 
     low_half = pair < pairs // 2
 
-    def close(q):
-        return jnp.where(low_half, plan[q][0], plan[q][1])
-
-    def owners(q):
-        other = jnp.where(low_half, plan[q][1], plan[q][0])
-        block = jnp.where(low_half, 2, 0)
-        own = 2 - block
-        return (
-            (other * 2, block),
-            (other * 2 + 1, block + 1),
-            (close(q) * 2 + 1 - side, own + 1 - side),
-            (close(q) * 2 + side, own + side),
-        )
-
-    def is_owner(q):
-        return pair == close(q)
-
-    def slot(q):
-        return owners(q)[3][1]
+    close = jnp.where(low_half, near[0], near[1])
+    away = jnp.where(low_half, near[1], near[0])
+    block = jnp.where(low_half, 2, 0)
+    owners = (
+        (away * 2, block),
+        (away * 2 + 1, block + 1),
+        (close * 2 + 1 - side, 2 - block + 1 - side),
+        (close * 2 + side, 2 - block + side),
+    )
+    slot = owners[3][1]
+    in_near = pair == close
+    outer = [2 * chip + core for chip in range(pairs) if chip not in near for core in range(2)]
+
+    def when_near(run):
+        pl.when(in_near)(run)
+
+    def when_outer(run):
+        pl.when(jnp.logical_not(in_near))(run)
+
+    def to_owners(do):
+        for k in range(size - 1):
+            do(k)
+        when_outer(lambda: do(size - 1))
 
     if pairs == 4:
         inward = jnp.where(low_half, pair + 1, pair - 1)
@@ -330,64 +328,64 @@
     barrier = pltpu.get_barrier_semaphore()
     for peer in peers:
         pl.semaphore_signal(barrier, inc=1, device_id={"clus": peer}, device_id_type=MESH)
-    for k in range(1, m):
-        pl.semaphore_signal(barrier, inc=1, device_id={"dp": dp_peer(k)}, device_id_type=MESH)
+    def greet(device):
+        pl.semaphore_signal(barrier, inc=1, device_id={"dp": device}, device_id_type=MESH)
+
+    to_owners(lambda k: greet(owners[k][0]))
+
+    @when_near
+    def _():
+        for device in outer:
+            greet(device)
+
     fetch = [
         pltpu.make_async_copy(src, dst, in_sem.at[i])
         for i, (src, dst) in enumerate(
-            [
+            (
                 (fa_hbm, fa_all.at[me]),
                 (p1_hbm, p1_all.at[me]),
                 (p2_hbm, p2_all.at[dp]),
                 (rows_ref, rows_own),
                 (p3_hbm, p3_ref),
                 (shrink_hbm, shrink_ref),
-            ]
+            )
         )
     ]
     for copy in fetch:
         copy.start()
-    pl.semaphore_wait(barrier, n - 1 + m - 1)
+    pl.semaphore_wait(barrier, n - 1 + jnp.where(in_near, m - 1, size))
     for copy in fetch[:3]:
         copy.wait()
 
-    id_copies = []
-    for k, peer in enumerate(peers):
+    for peer in peers:
         for which, ids in enumerate((fa_all, p1_all)):
             own = ids.at[me]
-            id_copies.append(
-                remote(own, own, id_send.at[which, k], id_recv.at[which, k], {"clus": peer})
-            )
-    start(id_copies)
-    start(
-        [
-            remote(
-                p2_all.at[dp], p2_all.at[dp], p2_send.at[k], p2_recv.at[dp], {"dp": dp_peer(k)}
-            )
-            for k in range(1, m)
-        ]
-    )
+            start([remote(own, own, id_send.at[which], id_recv.at[which], {"clus": peer})])
+
+    def p2_copy(k):
+        own = p2_all.at[dp]
+        return remote(own, own, p2_send, p2_recv, {"dp": owners[k][0]})
+
+    to_owners(lambda k: p2_copy(k).start())
     fetch[3].wait()
-    row_copies = []
     for q in range(chunks):
         t, a = divmod(q, 2)
         for p in range(n):
             lane = slice(p * share + t * LANES, p * share + (t + 1) * LANES)
             row_out[q, p] = halves(rows_own[0:some, lane], rows_own[some:count, lane], a)
-        row_copies.append(
-            start(
-                [
-                    remote(
-                        row_out.at[q, peer],
-                        row_in.at[q, span(me, some), :],
-                        row_send.at[q, k],
-                        row_recv.at[q, k],
-                        {"clus": peer},
-                    )
-                    for k, peer in enumerate(peers)
-                ]
-            )
-        )
+        start(
+            [
+                remote(
+                    row_out.at[q, peer],
+                    row_in.at[q, span(me, some), :],
+                    row_send,
+                    row_recv.at[q],
+                    {"clus": peer},
+                )
+                for peer in peers
+            ]
+        )
+    for q in range(chunks):
         row_in[q, span(me, some), :] = row_out[q, me]
 
     for copy in fetch[4:]:
@@ -397,28 +395,27 @@
     w2 = shrink_ref[2] * (total / (middle * m))
     w1 = shrink_ref[3] * (total / (fine_dev * devices))
     p3_row = p3_ref[...]
-    h4 = lanes_hot(column_of(p3_row), 0)
+    upper = lax.broadcasted_iota(jnp.int32, (third, LANES), 1) >= K4
+    h4 = jnp.where(upper, 1.0, lanes_hot(column_of(p3_row), 0).astype(F32)).astype(BF)
     h4f = rows_hot(LANES, p3_row)
     ones = jnp.ones((LANES, LANES), BF)
 
     def left_half(size):
         return lax.broadcasted_iota(jnp.int32, (size, LANES), 1) < HALF
 
-    def parents_of(i, own):
-        if not own:
-            block = p2_all.at[i]
-            remote(block, block, p2_send.at[0], p2_recv.at[i], {"dp": i}).wait_recv()
+    def parents_of(i):
         row = p2_all[i]
         ht[:, span(i, middle)] = rows_hot(third, row)
         p2_column = column_of(row)
         for j in range(0, third, LANES):
             hn[span(i, middle), j : j + LANES] = lanes_hot(p2_column, j)
 
-    parents_of(dp, True)
-    parents_of(pair * 2 + 1 - side, False)
-    parents_of(chips[0] * 2, False)
-    parents_of(chips[0] * 2 + 1, False)
-    arrive(id_copies)
+    @when_near
+    def _():
+        parents_of(dp)
+
+    landed(fa_all.at[0 : n - 1], id_recv.at[0])
+    landed(p1_all.at[0 : n - 1], id_recv.at[1])
     ids = [fa_all[i] for i in range(n)]
     ids = [x[:, 0:some] for x in ids] + [x[:, some:count] for x in ids]
     fa_row = jnp.concatenate(ids, axis=1) - dp * fine
@@ -433,44 +430,32 @@
     h2f[...] = rows_hot(middle, mid_row.astype(jnp.int32))
 
     def part_copy(q, k):
-        device, o = owners(q)[k]
+        device, o = owners[k]
         return remote(
             part_own.at[q, span(o, thin), :],
             part_all.at[q, dp],
-            part_send.at[q, k],
-            part_recv.at[q, dp],
+            part_send,
+            part_recv.at[q],
             {"dp": device},
         )
 
-    def part_from(q, i):
-        block = part_all.at[q, i]
-        return remote(block, block, part_send.at[q, 0], part_recv.at[q, i], {"dp": i})
-
     def cnt_copy(k):
-        peer = dp_peer(k)
-        return remote(cnt_own, cnt_all.at[dp], cnt_send.at[k], cnt_recv.at[dp], {"dp": peer})
-
-    def cnt_from(i):
-        return remote(cnt_own, cnt_all.at[i], cnt_send.at[0], cnt_recv.at[i], {"dp": i})
+        place = {"dp": owners[k][0]}
+        return remote(cnt_own, cnt_all.at[dp], cnt_send, cnt_recv, place)
 
     def sum_part(q):
-        arrive(row_copies[q])
+        landed(row_in.at[q, 0 : (n - 1) * some], row_recv.at[q])
         block = row_in[q]
         both = jnp.where(
             left_half(middle), dot(h2f[:, 0:packed], block), dot(h2f[:, packed:], block)
         )
         both = both + pltpu.roll(both, HALF, 1)
         part_own[q] = both.T[0:HALF].astype(BF)
-        for k in range(size - 1):
-            part_copy(q, k).start()
-
-        @pl.when(is_owner(q))
+        to_owners(lambda k: part_copy(q, k).start())
+
+        @when_near
         def _():
-            part_all[q, dp] = part_own[q, span(slot(q), thin), :]
-
-        @pl.when(jnp.logical_not(is_owner(q)))
-        def _():
-            part_copy(q, size - 1).start()
+            part_all[q, dp] = part_own[q, span(slot, thin), :]
 
         sums2[q] = both
 
@@ -479,21 +464,23 @@
         count2 = count2 + h2f[:, j : j + LANES]
     count2 = dot(count2, ones)
     cnt_own[...] = count2.T[0:1]
-    for k in range(1, m):
-        cnt_copy(k).start()
+    to_owners(lambda k: cnt_copy(k).start())
     cnt_all[dp] = cnt_own[...]
     sum_part(0)
-    for chip in chips[1:]:
-        parents_of(chip * 2, False)
-        parents_of(chip * 2 + 1, False)
+    @when_near
+    def _():
+        landed(p2_all.at[0 : m - 1], p2_recv)
+        for i in others:
+            parents_of(i)
+
 
     def back_copy(q, k):
         peer = others[k]
         return remote(
             back_own.at[q, :, span(peer, middle)],
-            back_all.at[q, span(slot(q), thin), :],
-            back_send.at[0, q, k],
-            back_recv.at[0, q, slot(q)],
+            back_all.at[q, span(slot, thin), :],
+            back_send.at[0],
+            back_recv.at[q],
             {"dp": peer},
         )
 
@@ -501,59 +488,34 @@
         peer = others[k]
         return remote(
             means3.at[q, :, span(peer // 2, window)],
-            coarse_all.at[q, span(slot(q), thin), :],
-            back_send.at[1, q, k],
-            back_recv.at[1, q, slot(q)],
+            coarse_all.at[q, span(slot, thin), :],
+            back_send.at[1],
+            coarse_recv.at[q // 2],
             {"dp": peer},
         )
 
-    def from_owners(which, q):
-        dst = (back_all, coarse_all)[which]
-
-        def wait(k):
-            device, o = owners(q)[k]
-            block = dst.at[q, span(o, thin), :]
-            send, recv = back_send.at[which, q, 0], back_recv.at[which, q, o]
-            remote(block, block, send, recv, {"dp": device}).wait_recv()
-
-        for k in range(size - 1):
-            wait(k)
-
-        @pl.when(jnp.logical_not(is_owner(q)))
-        def _():
-            wait(size - 1)
+    def from_owners(ref, sem):
+        when_near(lambda: landed(ref.at[:, 0 : (size - 1) * thin], sem))
+        when_outer(lambda: landed(ref, sem))
+
+    def third_counts():
+        landed(cnt_all.at[0 : m - 1], cnt_recv)
+        lines = jnp.concatenate([cnt_all[i] for i in range(m)], axis=1)
+        row = lax.broadcasted_iota(jnp.int32, (16, m * middle), 0)
+        stack = jnp.zeros((16, m * middle), F32)
+        for i, part in enumerate(pieces(lines, 3)):
+            stack = jnp.where(row == i, part.astype(F32), stack)
+        cnt3 = dot(stack.astype(BF), hn[...])
+        cnt3 = cnt3[0:1] + cnt3[1:2] + cnt3[2:3]
+        cnt_third[...] = cnt3
+        cnt_top[...] = dot_stack(jnp.broadcast_to(cnt3, (16, third)), h4)[0:1]
 
     def third_level(q):
-        total3 = jnp.zeros((thin + 16, third), F32)
-        if q == plan.index(plan[q]):
-            for i in others:
-                cnt_from(i).wait_recv()
-        for chip in (pair, *chips):
-            for i in (chip * 2, chip * 2 + 1) if chip is not pair else (pair * 2 + 1 - side,):
-                part_from(q, i).wait_recv()
-            block = jnp.concatenate([part_all[q, chip * 2 + c] for c in range(2)], axis=1)
-            if q == plan.index(plan[q]):
-                lines = jnp.concatenate([cnt_all[chip * 2 + c] for c in range(2)], axis=1)
-                row = lax.broadcasted_iota(jnp.int32, (16, 2 * middle), 0)
-                stack = jnp.zeros((16, 2 * middle), F32)
-                for i, part in enumerate(pieces(lines, 3)):
-                    stack = jnp.where(row == i, part.astype(F32), stack)
-                block = jnp.concatenate([block, stack.astype(BF)], axis=0)
-                total3 = total3 + dot(block, hn[span(chip, 2 * middle), :])
-            else:
-                total3 = total3[0:thin] + dot(block, hn[span(chip, 2 * middle), :])
-        sums3 = total3[0:thin]
-        if q == plan.index(plan[q]):
-            cnt3 = total3[thin : thin + 1] + total3[thin + 1 : thin + 2] + total3[thin + 2 : thin + 3]
-            cnt_third[...] = cnt3
-            both = jnp.concatenate([sums3, jnp.broadcast_to(cnt3, (16, third))], axis=0)
-            both = dot_stack(both, h4)
-            sums4, cnt4 = both[0:thin], both[thin : thin + 1]
-            cnt_top[...] = cnt4
-        else:
-            cnt3, cnt4 = cnt_third[...], cnt_top[...]
-            sums4 = dot_stack(sums3, h4)
-        center = jnp.sum(sums4, axis=1, keepdims=True) / total
+        landed(part_all.at[q, 0 : m - 1], part_recv.at[q])
+        sums3 = dot(jnp.concatenate([part_all[q, i] for i in range(m)], axis=1), hn[...])
+        sums4 = dot_stack(sums3, h4)
+        cnt3, cnt4 = cnt_third[...], cnt_top[...]
+        center = pltpu.roll(sums4, K4, 1) / total
         means4 = (sums4 + w4 * center) / (cnt4 + w4)
         block = ((sums3 + w3 * dot_stack(means4, h4f)) / (cnt3 + w3)).astype(BF)
         means3[q] = block
@@ -562,13 +524,11 @@
             back_copy(q, k).start()
         for k in range(m - 1):
             coarse_copy(q, k).start()
-        back_all[q, span(slot(q), thin), :] = back_own[q, :, span(dp, middle)]
-        coarse_all[q, span(slot(q), thin), :] = means3[q, :, span(dp // 2, window)]
+        back_all[q, span(slot, thin), :] = back_own[q, :, span(dp, middle)]
+        coarse_all[q, span(slot, thin), :] = means3[q, :, span(dp // 2, window)]
 
     def run_third(q):
-        @pl.when(is_owner(q))
-        def _():
-            third_level(q)
+        when_near(lambda: third_level(q))
 
     def unpack(t):
         a, b = row_in[2 * t], row_in[2 * t + 1]
@@ -581,32 +541,27 @@
             some_counts = some_counts + h1f[:, j : j + LANES]
         return dot(some_counts, ones)
 
-    def bases(t):
-        unpack(t)
+    def bases():
+        for t in range(tiles):
+            unpack(t)
         left = left_half(few)
-        if t == 0:
-            scale2[...] = 1.0 / (count2 + w2)
-            rate1[...] = 1.0 / (fine_counts() + w1)
-        sums1 = dot(h1f[...], got[:, tile_of(t)])
+        scale2[...] = 1.0 / (count2 + w2)
+        rate1 = 1.0 / (fine_counts() + w1)
+        sums1 = dot(h1f[...], got[...])
         for p in range(n):
             low = slice(p * fine_dev, p * fine_dev + few)
             high = slice(p * fine_dev + few, (p + 1) * fine_dev)
             place = slice(p * few, (p + 1) * few)
-            rate_a, rate_b = rate1[low], rate1[high]
-            if t == 0:
-                pull1[place, :] = w1 * jnp.where(left, rate_a, rate_b)
-            a = sums1[low] * rate_a
-            b = sums1[high] * rate_b
-            base1[2 * t, place, :] = halves(a, b, 0)
-            base1[2 * t + 1, place, :] = halves(a, b, 1)
-
-    fine_copies = []
-    mid_copies = []
-    local_copies = []
+            pull1[place, :] = w1 * jnp.where(left, rate1[low], rate1[high])
+            for t in range(tiles):
+                a = sums1[low, tile_of(t)] * rate1[low]
+                b = sums1[high, tile_of(t)] * rate1[high]
+                base1[2 * t, place, :] = halves(a, b, 0)
+                base1[2 * t + 1, place, :] = halves(a, b, 1)
 
     def down(q):
         t, a = divmod(q, 2)
-        from_owners(0, q)
+        from_owners(back_all.at[q : q + 1], back_recv.at[q])
         prior2 = back_all[q].astype(F32)
         prior2 = jnp.concatenate([prior2, prior2], axis=0).T
         means2 = (sums2[q] + w2 * prior2) * scale2[...]
@@ -618,42 +573,38 @@
             place = slice(p * few, (p + 1) * few)
             means1 = base1[q, place] + pull1[place] * jnp.where(left, low, high)
             fine_out[q, p] = means1.astype(BF)
-        copies = start(
+        start(
             [
                 remote(
                     fine_out.at[q, peer],
                     fine_in.at[q, me],
-                    fine_send.at[q, k],
-                    fine_recv.at[q, k],
+                    fine_send,
+                    fine_recv.at[t],
                     {"clus": peer},
                 )
                 for k, peer in enumerate(peers)
             ]
         )
-        fine_copies.append(copies)
         if not a:
             mid_half[...] = means2
             return
         mid_own[:, tile_of(t)] = jnp.where(left_half(middle), mid_half[...], means2).astype(BF)
-        for k, peer in enumerate(peers):
-            mid_copies.extend(
-                start(
-                    [
-                        remote(
-                            mid_own.at[span(peer, mid_share), tile_of(t)],
-                            mid_ref.at[:, column(me, t)],
-                            mid_send.at[t, k],
-                            mid_recv.at[t, k],
-                            {"clus": peer},
-                        )
-                    ]
+        start(
+            [
+                remote(
+                    mid_own.at[span(peer, mid_share), tile_of(t)],
+                    mid_ref.at[:, column(me, t)],
+                    mid_send,
+                    mid_recv,
+                    {"clus": peer},
                 )
-            )
+                for peer in peers
+            ]
+        )
         copy = pltpu.make_async_copy(
-            mid_own.at[span(me, mid_share), tile_of(t)], mid_ref.at[:, column(me, t)], local_sem.at[t]
+            mid_own.at[span(me, mid_share), tile_of(t)], mid_ref.at[:, column(me, t)], local_sem.at[0]
         )
         copy.start()
-        local_copies.append(copy)
 
     def rows_by_fine():
         fa_column = column_of(fa_row)
@@ -661,33 +612,23 @@
             h1r[:, j : j + LANES] = lanes_hot(fa_column, j)
 
     def coarse(t):
-        for q in (2 * t, 2 * t + 1):
-            from_owners(1, q)
+        from_owners(coarse_all.at[2 * t : 2 * t + 2], coarse_recv.at[t])
         block = jnp.concatenate([coarse_all[2 * t], coarse_all[2 * t + 1]], axis=0)
         coarse_own[:, tile_of(t)] = block.astype(F32).T.astype(BF)
 
         def place(peer):
             return coarse_own.at[span(side * n + peer, third_share), tile_of(t)]
 
-        out_copies.extend(
-            start(
-                [
-                    remote(
-                        place(peer),
-                        coarse_ref.at[:, column(me, t)],
-                        out_send.at[t, k],
-                        out_recv.at[t, k],
-                        {"clus": peer},
-                    )
-                    for k, peer in enumerate(peers)
-                ]
-            )
-        )
-        copy = pltpu.make_async_copy(
-            place(me), coarse_ref.at[:, column(me, t)], local_sem.at[tiles + t]
-        )
+        start(
+            [
+                remote(
+                    place(peer), coarse_ref.at[:, column(me, t)], out_send, out_recv, {"clus": peer}
+                )
+                for peer in peers
+            ]
+        )
+        copy = pltpu.make_async_copy(place(me), coarse_ref.at[:, column(me, t)], local_sem.at[1])
         copy.start()
-        local_copies.append(copy)
 
     def fine_tile(t):
         for p in range(n):
@@ -695,7 +636,6 @@
             fine_own[p * fine_dev : p * fine_dev + few, tile_of(t)] = halves(a, b, 0)
             fine_own[p * fine_dev + few : (p + 1) * fine_dev, tile_of(t)] = halves(a, b, 1)
 
-    out_copies = []
     p1_row = jnp.concatenate([p1_all[i] for i in range(n)], axis=1) - dp * middle
     p1_column = column_of(p1_row)
     for j in range(0, middle, LANES):
@@ -704,12 +644,11 @@
     h1f[...] = rows_hot(fine, fa_row)
     for q in range(2, chunks - 1):
         sum_part(q)
-    bases(0)
+    when_near(third_counts)
     run_third(0)
     sum_part(chunks - 1)
     run_third(1)
-    for t in range(1, tiles):
-        bases(t)
+    bases()
     run_third(2)
     down(0)
     for q in range(3, chunks):
@@ -742,58 +681,51 @@
     for i in range(n):
         err_own[i] = err_fine[:, i * fine_dev : (i + 1) * fine_dev]
         tally[i] = by_fine[3:4, i * fine_dev : (i + 1) * fine_dev]
-    err_copies = start(
+    start(
         [
-            remote(
-                err_own.at[peer],
-                err_all.at[me],
-                err_send.at[k],
-                err_recv.at[k],
-                {"clus": peer},
-            )
-            for k, peer in enumerate(peers)
+            remote(err_own.at[peer], err_all.at[me], err_send, err_recv, {"clus": peer})
+            for peer in peers
         ]
     )
     err_all[me] = err_own[me]
 
     for t in range(tiles):
-        for q in (2 * t, 2 * t + 1):
-            arrive(fine_copies[q])
+        landed(fine_in.at[2 * t : 2 * t + 2, 0 : n - 1], fine_recv.at[t])
         for k in range(1, n):
             peer = lax.rem(me + k, n)
             a, b = fine_in[2 * t, peer], fine_in[2 * t + 1, peer]
             fine_ref[0:few, column(peer, t)] = halves(a, b, 0)
             fine_ref[few:, column(peer, t)] = halves(a, b, 1)
-    arrive(err_copies)
+    landed(err_all.at[0 : n - 1], err_recv)
     err = err_all[0]
     for i in range(1, n):
         err = err + err_all[i]
     spread_ref[...] = err / (width * (tally[me] + 1.0))
-    for copy in local_copies:
-        copy.wait()
-    arrive(mid_copies)
-    arrive(out_copies)
-    for copy in started:
-        copy.wait_send()
-    for k in range(1, m):
-        cnt_copy(k).wait_send()
-    for q in range(chunks):
-        for k in range(size - 1):
-            part_copy(q, k).wait_send()
-
-    def drain(q):
-        @pl.when(is_owner(q))
-        def _():
-            for k in range(m - 1):
-                back_copy(q, k).wait_send()
-                coarse_copy(q, k).wait_send()
-
-        @pl.when(jnp.logical_not(is_owner(q)))
-        def _():
-            part_copy(q, size - 1).wait_send()
-
-    for q in range(chunks):
-        drain(q)
+    landed(mid_ref.at[:, 0:share], local_sem.at[0])
+    landed(coarse_ref.at[:, 0:share], local_sem.at[1])
+    landed(mid_ref.at[:, 0 : (n - 1) * share], mid_recv)
+    landed(coarse_ref.at[:, 0 : (n - 1) * share], out_recv)
+    landed(fa_all.at[0 : n - 1], id_send.at[0])
+    landed(p1_all.at[0 : n - 1], id_send.at[1])
+    landed(row_out.at[:, 0 : n - 1], row_send)
+    landed(fine_out.at[:, 0 : n - 1], fine_send)
+    landed(mid_own.at[0 : (n - 1) * mid_share], mid_send)
+    landed(coarse_own.at[0 : (n - 1) * third_share], out_send)
+    landed(err_own.at[0 : n - 1], err_send)
+
+    @when_outer
+    def _():
+        landed(p2_all.at[0:size], p2_send)
+        landed(cnt_all.at[0:size], cnt_send)
+        landed(part_own, part_send)
+
+    @when_near
+    def _():
+        landed(p2_all.at[0 : size - 1], p2_send)
+        landed(cnt_all.at[0 : size - 1], cnt_send)
+        landed(part_own.at[:, 0 : (size - 1) * thin], part_send)
+        landed(back_own.at[:, :, 0 : (m - 1) * middle], back_send.at[0])
+        landed(back_own.at[:, :, 0 : (m - 1) * window], back_send.at[1])
 
 
 def land(count, *refs):
@@ -869,7 +801,6 @@
             pltpu.VMEM((chunks, fine // 2, LANES), F32),
             pltpu.VMEM((fine // 2, LANES), F32),
             pltpu.VMEM((middle, LANES), F32),
-            pltpu.VMEM((fine, LANES), F32),
             pltpu.VMEM((chunks, HALF, middle), BF),
             pltpu.VMEM((chunks, m, HALF // 4, middle), BF),
             pltpu.VMEM((1, middle), F32),
@@ -890,27 +821,28 @@
             pltpu.VMEM((n, 1, fine_dev), F32),
             pltpu.VMEM((n, 1, fine_dev), F32),
             dma((6,)),
-            dma((2, n)),
-            dma((2, n)),
-            dma((m,)),
-            dma((m,)),
-            dma((chunks, n)),
-            dma((chunks, n)),
-            dma((chunks, 4)),
-            dma((chunks, m)),
-            dma((m,)),
-            dma((m,)),
-            dma((2, chunks, m)),
-            dma((2, chunks, 4)),
-            dma((chunks, n)),
-            dma((chunks, n)),
-            dma((tiles, n)),
-            dma((tiles, n)),
-            dma((tiles, n)),
-            dma((tiles, n)),
-            dma((n,)),
-            dma((n,)),
-            dma((2 * tiles,)),
+            dma((2,)),
+            dma((2,)),
+            dma,
+            dma,
+            dma,
+            dma((chunks,)),
+            dma,
+            dma((chunks,)),
+            dma,
+            dma,
+            dma((2,)),
+            dma((chunks,)),
+            dma((tiles,)),
+            dma,
+            dma((tiles,)),
+            dma,
+            dma,
+            dma,
+            dma,
+            dma,
+            dma,
+            dma((2,)),
         ],
         compiler_params=pltpu.CompilerParams(
             collective_id=0, has_side_effects=True, vmem_limit_bytes=40 << 20
@@ -932,15 +864,15 @@
     n = lax.axis_size("clus")
     m = lax.axis_size("dp")
     return (
-        rows.shape[1] % (n * LANES) == 0
-        and m % 2 == 0
-        and m >= 4
+        rows.shape[1] == 2 * n * LANES
+        and m % 4 == 0
         and rows.shape[0] % (2 * LANES) == 0
-        and parent1.shape[0] % LANES == 0
+        and parent1.shape[0] % (2 * LANES) == 0
         and parent2.shape[0] % LANES == 0
         and parent2.shape[0] <= 256
         and parent2.shape[0] % (n * 16) == 0
         and parent3.shape[0] % (m // 2 * LANES) == 0
+        and parent3.shape[0] // (m // 2) <= parent2.shape[0]
         and parent3.shape[0] % (n * m * 16) == 0
     )
 

time: 33.4 us -> 30.4 us (0.910)
  Pallas kernels: 32.5 us -> 29.6 us
    pallas_call x1, Pallas kernels: 31.6 us -> 28.8 us  [fused(): pl.pallas_call(functools.partial(sweep, n, m), out_shape=(jax.ShapeDtypeS...]
where the time goes in v2:
time: 30.4 us; the launch traced here: 30.3 us
  Pallas kernels  29.6 us (97%)
  between operations  0.64 us (2%)
    pallas_call x1, Pallas kernels, fused(): pl.pallas_call(functools.partial(sweep, n, m), out_shape=(jax.ShapeDtypeS...  28.8 us
    pallas_call x1, Pallas kernels, settle(): pl.pallas_call(functools.partial(land, count), out_shape=tuple((jax.Shape...  0.87 us

profile of v2, /device:TPU:0, one launch (start us, length us, event | category | flops | bytes accessed | tf_op | source)
XLA Modules:
  0.0 30.3 jit_solution(7360820568959741667)
XLA Ops:
  0.6 28.8 %sweep.1 = (bf16[256,1024]{1,0:T(8,128)(2,1)S(1)}, bf16[64,1024]{1,0:T(8,128)(2,1)S(1)}, bf16[16,1024]{1,0:T(8,128)(2,1)S(1)}, f32[1,256]{1,0:T(1,128)S(1)}) custom-call(s32[1,256]{1,0:T(1,128)} %bitcast.6, s32[1,256]{1,0:T(1,128)} %bitcast.7, s32[1,256]{1,0:T(1,128)} %bitcast.8, s32[1,512]{1,0:T(1,128)} %bitcast.5, f32[4]{0:T(128)} %shrink_hbm.1, ...), custom_call_target="tpu_custom_call" | custom-call | tf_op jit(solution)/shard_map/sweep/pallas_call | solution.py:774
  29.4 0.9 %settle.1 = (bf16[256,1024]{1,0:T(8,128)(2,1)}, bf16[64,1024]{1,0:T(8,128)(2,1)}, bf16[16,1024]{1,0:T(8,128)(2,1)}, f32[1,256]{1,0:T(1,128)}) custom-call(bf16[256,1024]{1,0:T(8,128)(2,1)S(1)} %get-tuple-element.12.refs_0_, bf16[64,1024]{1,0:T(8,128)(2,1)S(1)} %get-tuple-element.13.refs_1_, bf16[16,1024]{1,0:T(8,128)(2,1)S(1)} %get-tuple-element.14.refs_2_, ...), custom_call_target="tpu_custom_call" | custom-call | tf_op jit(solution)/shard_map/settle/pallas_call | solution.py:743

commit v3 on v2

--- a/solution.py
+++ b/solution.py
@@ -190,6 +190,7 @@
     base1,
     pull1,
     scale2,
+    rate1,
     part_own,
     part_all,
     cnt_own,
@@ -541,18 +542,25 @@
             some_counts = some_counts + h1f[:, j : j + LANES]
         return dot(some_counts, ones)
 
-    def bases():
-        for t in range(tiles):
-            unpack(t)
+    def rates():
         left = left_half(few)
         scale2[...] = 1.0 / (count2 + w2)
-        rate1 = 1.0 / (fine_counts() + w1)
+        rate = 1.0 / (fine_counts() + w1)
+        rate1[...] = rate
+        for p in range(n):
+            low = rate[p * fine_dev : p * fine_dev + few]
+            high = rate[p * fine_dev + few : (p + 1) * fine_dev]
+            pull1[p * few : (p + 1) * few, :] = w1 * jnp.where(left, low, high)
+        unpack(0)
+
+    def bases():
+        for t in range(1, tiles):
+            unpack(t)
         sums1 = dot(h1f[...], got[...])
         for p in range(n):
             low = slice(p * fine_dev, p * fine_dev + few)
             high = slice(p * fine_dev + few, (p + 1) * fine_dev)
             place = slice(p * few, (p + 1) * few)
-            pull1[place, :] = w1 * jnp.where(left, rate1[low], rate1[high])
             for t in range(tiles):
                 a = sums1[low, tile_of(t)] * rate1[low]
                 b = sums1[high, tile_of(t)] * rate1[high]
@@ -565,7 +573,8 @@
         prior2 = back_all[q].astype(F32)
         prior2 = jnp.concatenate([prior2, prior2], axis=0).T
         means2 = (sums2[q] + w2 * prior2) * scale2[...]
-        prior1 = sum(dot(h1m[...], part) for part in pieces(means2, 2))
+        prior1 = dot(h1m[...], jnp.concatenate(pieces(means2, 2), axis=1))
+        prior1 = prior1[:, 0:LANES] + prior1[:, LANES:]
         left = left_half(few)
         for p in range(n):
             low = prior1[p * fine_dev : p * fine_dev + few]
@@ -642,6 +651,7 @@
         h1m[:, j : j + LANES] = lanes_hot(p1_column, j)
     sum_part(1)
     h1f[...] = rows_hot(fine, fa_row)
+    rates()
     for q in range(2, chunks - 1):
         sum_part(q)
     when_near(third_counts)
@@ -655,9 +665,9 @@
         run_third(q)
     for q in range(1, chunks):
         down(q)
-        if q % 2 and q < chunks - 1:
-            coarse(q // 2)
-            fine_tile(q // 2)
+        if q == chunks - 2:
+            coarse(0)
+            fine_tile(0)
             rows_by_fine()
     if chunks == 2:
         rows_by_fine()
@@ -801,6 +811,7 @@
             pltpu.VMEM((chunks, fine // 2, LANES), F32),
             pltpu.VMEM((fine // 2, LANES), F32),
             pltpu.VMEM((middle, LANES), F32),
+            pltpu.VMEM((fine, LANES), F32),
             pltpu.VMEM((chunks, HALF, middle), BF),
             pltpu.VMEM((chunks, m, HALF // 4, middle), BF),
             pltpu.VMEM((1, middle), F32),

time: 30.4 us -> 29.9 us (0.984)
  Pallas kernels: 29.6 us -> 29.1 us
    pallas_call x1, Pallas kernels: 28.8 us -> 28.2 us  [fused(): pl.pallas_call(functools.partial(sweep, n, m), out_shape=(jax.ShapeDtypeS...]
where the time goes in v3:
time: 29.9 us; the launch traced here: 29.8 us
  Pallas kernels  29.1 us (97%)
  between operations  0.64 us (2%)
    pallas_call x1, Pallas kernels, fused(): pl.pallas_call(functools.partial(sweep, n, m), out_shape=(jax.ShapeDtypeS...  28.2 us
    pallas_call x1, Pallas kernels, settle(): pl.pallas_call(functools.partial(land, count), out_shape=tuple((jax.Shape...  0.87 us

profile of v3, /device:TPU:0, one launch (start us, length us, event | category | flops | bytes accessed | tf_op | source)
XLA Modules:
  0.0 29.8 jit_solution(7065591331068509454)
XLA Ops:
  0.6 28.2 %sweep.1 = (bf16[256,1024]{1,0:T(8,128)(2,1)S(1)}, bf16[64,1024]{1,0:T(8,128)(2,1)S(1)}, bf16[16,1024]{1,0:T(8,128)(2,1)S(1)}, f32[1,256]{1,0:T(1,128)S(1)}) custom-call(s32[1,256]{1,0:T(1,128)} %bitcast.6, s32[1,256]{1,0:T(1,128)} %bitcast.7, s32[1,256]{1,0:T(1,128)} %bitcast.8, s32[1,512]{1,0:T(1,128)} %bitcast.5, f32[4]{0:T(128)} %shrink_hbm.1, ...), custom_call_target="tpu_custom_call" | custom-call | tf_op jit(solution)/shard_map/sweep/pallas_call | solution.py:784
  28.9 0.9 %settle.1 = (bf16[256,1024]{1,0:T(8,128)(2,1)}, bf16[64,1024]{1,0:T(8,128)(2,1)}, bf16[16,1024]{1,0:T(8,128)(2,1)}, f32[1,256]{1,0:T(1,128)}) custom-call(bf16[256,1024]{1,0:T(8,128)(2,1)S(1)} %get-tuple-element.12.refs_0_, bf16[64,1024]{1,0:T(8,128)(2,1)S(1)} %get-tuple-element.13.refs_1_, bf16[16,1024]{1,0:T(8,128)(2,1)S(1)} %get-tuple-element.14.refs_2_, ...), custom_call_target="tpu_custom_call" | custom-call | tf_op jit(solution)/shard_map/settle/pallas_call | solution.py:753

commit v4 on v3

--- a/solution.py
+++ b/solution.py
@@ -195,8 +195,8 @@
     part_all,
     cnt_own,
     cnt_all,
-    cnt_third,
-    cnt_top,
+    rate3,
+    rate4,
     means3,
     back_own,
     back_all,
@@ -280,7 +280,7 @@
         )
 
     if n == 4:
-        peers = [n - 1 - me, lax.rem(me + 2, n), me + 1 - 2 * lax.rem(me, 2)]
+        peers = [n - 1 - me, jnp.where(side == 0, lax.rem(me + 2, n), me + 1 - 2 * lax.rem(me, 2)), jnp.where(side == 0, me + 1 - 2 * lax.rem(me, 2), lax.rem(me + 2, n))]
     else:
         peers = [lax.rem(me + k, n) for k in range(1, n)]
 
@@ -354,6 +354,16 @@
     ]
     for copy in fetch:
         copy.start()
+
+    def pack(q):
+        t, a = divmod(q, 2)
+        for p in range(n):
+            lane = slice(p * share + t * LANES, p * share + (t + 1) * LANES)
+            row_out[q, p] = halves(rows_own[0:some, lane], rows_own[some:count, lane], a)
+
+    fetch[3].wait()
+    for q in range(1):
+        pack(q)
     pl.semaphore_wait(barrier, n - 1 + jnp.where(in_near, m - 1, size))
     for copy in fetch[:3]:
         copy.wait()
@@ -368,12 +378,9 @@
         return remote(own, own, p2_send, p2_recv, {"dp": owners[k][0]})
 
     to_owners(lambda k: p2_copy(k).start())
-    fetch[3].wait()
     for q in range(chunks):
-        t, a = divmod(q, 2)
-        for p in range(n):
-            lane = slice(p * share + t * LANES, p * share + (t + 1) * LANES)
-            row_out[q, p] = halves(rows_own[0:some, lane], rows_own[some:count, lane], a)
+        if q >= 1:
+            pack(q)
         start(
             [
                 remote(
@@ -450,15 +457,15 @@
         both = jnp.where(
             left_half(middle), dot(h2f[:, 0:packed], block), dot(h2f[:, packed:], block)
         )
-        both = both + pltpu.roll(both, HALF, 1)
-        part_own[q] = both.T[0:HALF].astype(BF)
+        turned = both.T
+        part_own[q] = (turned[0:HALF] + turned[HALF:]).astype(BF)
         to_owners(lambda k: part_copy(q, k).start())
 
         @when_near
         def _():
             part_all[q, dp] = part_own[q, span(slot, thin), :]
 
-        sums2[q] = both
+        sums2[q] = both + pltpu.roll(both, HALF, 1)
 
     count2 = h2f[:, 0:LANES]
     for j in range(LANES, n * count, LANES):
@@ -508,17 +515,17 @@
             stack = jnp.where(row == i, part.astype(F32), stack)
         cnt3 = dot(stack.astype(BF), hn[...])
         cnt3 = cnt3[0:1] + cnt3[1:2] + cnt3[2:3]
-        cnt_third[...] = cnt3
-        cnt_top[...] = dot_stack(jnp.broadcast_to(cnt3, (16, third)), h4)[0:1]
+        rate3[...] = 1.0 / (cnt3 + w3)
+        cnt4 = dot_stack(jnp.broadcast_to(cnt3, (16, third)), h4)[0:1]
+        rate4[...] = 1.0 / (cnt4 + w4)
 
     def third_level(q):
         landed(part_all.at[q, 0 : m - 1], part_recv.at[q])
         sums3 = dot(jnp.concatenate([part_all[q, i] for i in range(m)], axis=1), hn[...])
         sums4 = dot_stack(sums3, h4)
-        cnt3, cnt4 = cnt_third[...], cnt_top[...]
         center = pltpu.roll(sums4, K4, 1) / total
-        means4 = (sums4 + w4 * center) / (cnt4 + w4)
-        block = ((sums3 + w3 * dot_stack(means4, h4f)) / (cnt3 + w3)).astype(BF)
+        means4 = (sums4 + w4 * center) * rate4[...]
+        block = ((sums3 + w3 * dot_stack(means4, h4f)) * rate3[...]).astype(BF)
         means3[q] = block
         back_own[q] = dot(block, ht[...]).astype(BF)
         for k in range(m - 1):

time: 29.9 us -> 29.9 us (level)
  no operation moved by 1% of the time
where the time goes in v4:
time: 29.9 us; the launch traced here: 29.7 us
  Pallas kernels  29.1 us (97%)
  between operations  0.64 us (2%)
    pallas_call x1, Pallas kernels, fused(): pl.pallas_call(functools.partial(sweep, n, m), out_shape=(jax.ShapeDtypeS...  28.2 us
    pallas_call x1, Pallas kernels, settle(): pl.pallas_call(functools.partial(land, count), out_shape=tuple((jax.Shape...  0.87 us

profile of v4, /device:TPU:0, one launch (start us, length us, event | category | flops | bytes accessed | tf_op | source)
XLA Modules:
  0.0 29.7 jit_solution(5051201197339645470)
XLA Ops:
  0.6 28.2 %sweep.1 = (bf16[256,1024]{1,0:T(8,128)(2,1)S(1)}, bf16[64,1024]{1,0:T(8,128)(2,1)S(1)}, bf16[16,1024]{1,0:T(8,128)(2,1)S(1)}, f32[1,256]{1,0:T(1,128)S(1)}) custom-call(s32[1,256]{1,0:T(1,128)} %bitcast.6, s32[1,256]{1,0:T(1,128)} %bitcast.7, s32[1,256]{1,0:T(1,128)} %bitcast.8, s32[1,512]{1,0:T(1,128)} %bitcast.5, f32[4]{0:T(128)} %shrink_hbm.1, ...), custom_call_target="tpu_custom_call" | custom-call | tf_op jit(solution)/shard_map/sweep/pallas_call | solution.py:791
  28.9 0.9 %settle.1 = (bf16[256,1024]{1,0:T(8,128)(2,1)}, bf16[64,1024]{1,0:T(8,128)(2,1)}, bf16[16,1024]{1,0:T(8,128)(2,1)}, f32[1,256]{1,0:T(1,128)}) custom-call(bf16[256,1024]{1,0:T(8,128)(2,1)S(1)} %get-tuple-element.12.refs_0_, bf16[64,1024]{1,0:T(8,128)(2,1)S(1)} %get-tuple-element.13.refs_1_, bf16[16,1024]{1,0:T(8,128)(2,1)S(1)} %get-tuple-element.14.refs_2_, ...), custom_call_target="tpu_custom_call" | custom-call | tf_op jit(solution)/shard_map/settle/pallas_call | solution.py:760
